TPU v7x, 256 devices: a whole 4x4x8 slice. The times are simulated.
256 devices in a mesh: gz: 8 (over y, z_lo), ta: 32 (over z_hi, x, core).
Axes of the slice: x: 4, y: 4, z: 8 (z_hi: 4, z_lo: 2; z = z_hi * 2 + z_lo), core: 2. Of those that a mesh axis runs over, the one named last changes fastest.
Arguments:
- raw_planes: float32 [256, 2, 320, 2048], P(('gz', 'ta')), may hold values from 10 to 8000, as said below
- offsets: int32 [256, 2], replicated, may hold values from 0 to 63
Outputs:
- corrected: float32 [256, 2, 320, 2048], P(('gz', 'ta'))
- east_corr: float32 [256, 320, 256], P(('gz', 'ta'))
- south_corr: float32 [256, 256, 2048], P(('gz', 'ta'))
Inputs may be any that keep to these rules, and one draw needn't show every extreme that they name: `raw_planes`: counts are positive.
All inputs are finite; a program needn't handle non-finite values.
Results may differ from a plain program's by a relative error of at most 0.0003.
Values sent between devices are 32-bit elements; how exact they have to be, the bound alone decides.
A program may use at most 128 MiB of HBM per device.

v0:
```python
import math

import jax
import jax.numpy as jnp
from jax import lax
from jax.sharding import PartitionSpec as P

INTERSECTION = 256
GRID_COLS = 8


HIGHEST = lax.Precision.HIGHEST


def cut_along(x, dim, length):
    shape = x.shape
    tiles = x.reshape(*shape[:dim], length, shape[dim] // length, *shape[dim + 1 :])
    return jnp.moveaxis(tiles, dim, 0)


def one_scatter(arrays, axis, dims):
    length = lax.axis_size(axis)
    tiles = [cut_along(a, dim, length) for a, dim in zip(arrays, dims)]
    lines = jnp.concatenate([b.reshape(length, -1) for b in tiles], axis=1)
    extent = max(16, -(-lines.shape[1] // 1024) * 8)
    lines = jnp.pad(lines, ((0, 0), (0, extent * 128 - lines.shape[1]))).reshape(-1, 128)
    vector, at, outs = (lax.psum_scatter(lines, axis, tiled=True).reshape(-1), 0, [])
    for b in tiles:
        part = b[0]
        outs.append(vector[at : at + part.size].reshape(part.shape))
        at += part.size
    return tuple(outs)


def copy_for_each(x, axis):
    copies = jnp.broadcast_to(x, (lax.axis_size(axis), *x.shape))
    return lax.all_to_all(copies, axis, split_axis=0, concat_axis=0, tiled=True)


def taken_together(x, axis):
    return copy_for_each(x, axis).sum(axis=0)


def together(arrays, axis):
    vector, at, outs = (jnp.concatenate([a.reshape(-1) for a in arrays]), 0, [])
    total = taken_together(vector, axis)
    for a in arrays:
        outs.append(total[at : at + a.size].reshape(a.shape))
        at += a.size
    return tuple(outs)


def sent_together(arrays, axis, dim, along):
    both = jnp.concatenate(arrays, axis=along)
    out, at, outs = (lax.all_gather(both, axis, axis=dim, tiled=True), 0, [])
    for a in arrays:
        outs.append(lax.slice_in_dim(out, at, at + a.shape[along], axis=along))
        at += a.shape[along]
    return tuple(outs)


def shifted(value, axis, steps):
    count = lax.axis_size(axis)
    first, last = (max(0, -steps), min(count, count - steps))
    return lax.ppermute(value, axis, [(source, source + steps) for source in range(first, last)])


def contract(pattern, left, right):
    return jnp.einsum(pattern, left, right, precision=HIGHEST)


def dft_table(length):
    counter = jnp.arange(length, dtype=jnp.int32)
    product = counter[:, None] * counter[None, :] % length
    angle = product.astype(jnp.float32) * (2.0 * math.pi / length)
    return (jnp.cos(angle), jnp.sin(angle))


def twiddle_table(first, second):
    length = first * second
    product = (
        jnp.arange(first, dtype=jnp.int32)[:, None]
        * jnp.arange(second, dtype=jnp.int32)[None, :]
        % length
    )
    angle = product.astype(jnp.float32) * (2.0 * math.pi / length)
    return (jnp.cos(angle), jnp.sin(angle))


def make_plan(rows_count, cols_count):
    second = min(cols_count, 128)
    first = cols_count // second
    return (
        dft_table(rows_count),
        dft_table(first),
        twiddle_table(first, second),
        dft_table(second),
        first,
        second,
    )


def forward(strip, plan):
    rows_table, first_table, twist_table, second_table, first, second = plan
    rows_count, cols_count = strip.shape
    real_part = contract("ab,bc->ac", rows_table[0], strip).reshape(rows_count, first, second)
    imag_part = (-contract("ab,bc->ac", rows_table[1], strip)).reshape(rows_count, first, second)
    section_re = contract("ab,mbn->man", first_table[0], real_part) + contract(
        "ab,mbn->man", first_table[1], imag_part
    )
    section_im = contract("ab,mbn->man", first_table[0], imag_part) - contract(
        "ab,mbn->man", first_table[1], real_part
    )
    turned_re = section_re * twist_table[0] + section_im * twist_table[1]
    turned_im = section_im * twist_table[0] - section_re * twist_table[1]
    spec_re = contract("man,nk->mak", turned_re, second_table[0]) + contract(
        "man,nk->mak", turned_im, second_table[1]
    )
    spec_im = contract("man,nk->mak", turned_im, second_table[0]) - contract(
        "man,nk->mak", turned_re, second_table[1]
    )
    return (spec_re, spec_im)


def inverse_real(spec_re, spec_im, plan):
    rows_table, first_table, twist_table, second_table, first, second = plan
    rows_count = spec_re.shape[0]
    back_re = contract("mak,kn->man", spec_re, second_table[0]) - contract(
        "mak,kn->man", spec_im, second_table[1]
    )
    back_im = contract("mak,kn->man", spec_im, second_table[0]) + contract(
        "mak,kn->man", spec_re, second_table[1]
    )
    turned_re = back_re * twist_table[0] - back_im * twist_table[1]
    turned_im = back_im * twist_table[0] + back_re * twist_table[1]
    pixel_re = contract("ab,mbn->man", first_table[0], turned_re) - contract(
        "ab,mbn->man", first_table[1], turned_im
    )
    pixel_im = contract("ab,mbn->man", first_table[0], turned_im) + contract(
        "ab,mbn->man", first_table[1], turned_re
    )
    pixel_re = pixel_re.reshape(rows_count, first * second)
    pixel_im = pixel_im.reshape(rows_count, first * second)
    return contract("ab,bc->ac", rows_table[0], pixel_re) - contract(
        "ab,bc->ac", rows_table[1], pixel_im
    )


def correlate(own_strip, other_strip):
    rows_count, cols_count = own_strip.shape
    plan = make_plan(rows_count, cols_count)
    own_re, own_im = forward(own_strip, plan)
    other_re, other_im = forward(other_strip, plan)
    cross_re = own_re * other_re + own_im * other_im
    cross_im = own_im * other_re - own_re * other_im
    magnitude = jnp.sqrt(cross_re * cross_re + cross_im * cross_im)
    weight = 1.0 / (magnitude + jnp.mean(magnitude) + 1e-06)
    surface = inverse_real(cross_re * weight, cross_im * weight, plan)
    return surface / math.sqrt(rows_count * cols_count)


def body(raw_planes, offsets):
    tile_stack = raw_planes[0]
    plane_count = tile_stack.shape[0]
    rows_count = tile_stack.shape[1]
    width_count = tile_stack.shape[2]
    count_ta = lax.axis_size("ta")
    tiles_all = lax.axis_size("gz") * count_ta
    slot = lax.axis_index("ta")
    own_tile = lax.axis_index("gz") * count_ta + slot
    has_east = slot < count_ta - 1
    has_north = slot >= GRID_COLS
    log_planes = jnp.log(tile_stack)
    log_sum = jnp.sum(log_planes, 0)
    min_sum = jnp.min(log_planes, 0)
    own_east = offsets[own_tile, 0]
    own_south = offsets[own_tile, 1]
    west_mean = jnp.mean(tile_stack[:, :, :INTERSECTION], 0)
    shares = one_scatter((log_sum, min_sum), "ta", (0, 0))
    shares = together((shares[0], shares[1]), "gz")
    log_total, min_total = sent_together((shares[0], shares[1]), "ta", 0, 1)
    flat_field = jnp.exp(log_total / (tiles_all * plane_count))
    dark_field = 0.5 * jnp.exp(min_total / tiles_all)
    flat_field, dark_field = (flat_field, dark_field)
    west_ready = (west_mean - dark_field[:, :INTERSECTION]) / flat_field[:, :INTERSECTION]
    start = rows_count - INTERSECTION - own_south
    strip = jnp.mean(lax.dynamic_slice_in_dim(tile_stack, start, INTERSECTION, 1), 0)
    south_start = rows_count - INTERSECTION - own_south
    dark_part = lax.dynamic_slice_in_dim(dark_field, south_start, INTERSECTION, 0)
    flat_part = lax.dynamic_slice_in_dim(flat_field, south_start, INTERSECTION, 0)
    south_ready = (strip - dark_part) / flat_part
    east_partner = shifted(west_ready, "ta", -1)
    north_partner = shifted(south_ready, "ta", GRID_COLS)
    east_partner = jnp.where(has_east, east_partner, 0.0)
    north_partner = jnp.where(has_north, north_partner, 0.0)
    corrected = (tile_stack - dark_field) / flat_field
    start = width_count - INTERSECTION - own_east
    strip = jnp.mean(lax.dynamic_slice_in_dim(tile_stack, start, INTERSECTION, 2), 0)
    east_start = width_count - INTERSECTION - own_east
    dark_part = lax.dynamic_slice_in_dim(dark_field, east_start, INTERSECTION, 1)
    flat_part = lax.dynamic_slice_in_dim(flat_field, east_start, INTERSECTION, 1)
    own_eastern = (strip - dark_part) / flat_part
    own_north = (
        jnp.mean(tile_stack[:, :INTERSECTION, :], 0) - dark_field[:INTERSECTION, :]
    ) / flat_field[:INTERSECTION, :]
    east_corr = correlate(own_eastern, east_partner)
    south_corr = correlate(own_north, north_partner)
    return (corrected[None], east_corr[None], south_corr[None])


def solution(mesh):
    in_specs = (P(("gz", "ta"), None, None, None), P())
    out_specs = (
        P(("gz", "ta"), None, None, None),
        P(("gz", "ta"), None, None),
        P(("gz", "ta"), None, None),
    )
    return jax.shard_map(body, mesh=mesh, in_specs=in_specs, out_specs=out_specs, check_vma=False)
```

profile of v0, /device:TPU:98, one launch (start us, length us, event | category | flops | bytes accessed | tf_op | source)
XLA Modules:
  0.0 460.6 jit_solution(13532019451831207696)
XLA Ops:
  7.2 7.7 %log_reduce_fusion.1 = (f32[320,2048]{1,0:T(8,128)}, f32[320,2048]{1,0:T(8,128)}) fusion(f32[1,2,320,2048]{3,2,1,0:T(8,128)} %param.2), kind=kLoop, calls=%fused_computation.3 | loop fusion | flops 1310720 | bytes 10485760 | tf_op jit(solution)/shard_map/reduce_sum | solution.py:174
  17.5 3.6 reshape_reshape.7
  21.1 4.5 pad_maximum_fusion
  25.6 5.5 %reshape.154 = f32[10240,128]{1,0:T(8,128)} reshape(f32[32,40960]{1,0:T(8,128)} %pad_maximum_fusion) | data formatting | bytes 10485760 | tf_op jit(solution)/shard_map/reshape | solution.py:26
  31.2 104.2 %reduce-scatter.2.cloned.1.call-done = f32[320,128]{1,0:T(8,128)} async-done(((f32[10240,128]{1,0:T(8,128)}), f32[320,128]{1,0:T(8,128)}) %reduce-scatter.2.cloned.1.call-update) | async-done | bytes 163856 | tf_op jit(solution)/shard_map/reduce_scatter | solution.py:27
  137.1 21.5 %all_to_all.6 = f32[8,1,40960]{2,1,0:T(1,128)S(1)} all-to-all(f32[8,1,40960]{2,1,0:T(1,128)S(1)} %broadcast_in_dim.14), channel_id=1, replica_groups=mesh['gz'=8,'ta'=32] {'gz'}, dimensions={0} | all-to-all | bytes 2621440 | tf_op jit(solution)/shard_map/all_to_all | solution.py:37
  171.9 64.3 %all-gather.3.cloned.1.call-done = f32[32,10,4096]{2,1,0:T(8,128)} async-done(((f32[1,10,4096]{2,1,0:T(8,128)}), f32[32,10,4096]{2,1,0:T(8,128)}) %all-gather.3.cloned.1.call-update) | async-done | bytes 5242896 | tf_op jit(solution)/shard_map/all_gather | solution.py:55
  236.2 6.2 %reshape.168 = f32[320,4096]{1,0:T(8,128)} reshape(f32[32,10,4096]{2,1,0:T(8,128)} %all-gather.3.cloned.1.call-done) | data formatting | bytes 10485760
  242.4 3.3 fusion.4
  252.5 4.4 convolution_bitcast_fusion
  256.9 4.4 fusion.65
  261.4 3.5 subtract_divide_fusion
  281.2 3.3 convolution_add_fusion.2
  284.6 3.5 collective-permute-start.1
  288.1 3.3 convolution_subtract_fusion.3
  321.7 3.6 fusion.71
  325.3 55.1 %collective-permute-done.1 = f32[256,2048]{1,0:T(8,128)S(1)} collective-permute-done((f32[256,2048]{1,0:T(8,128)}, f32[256,2048]{1,0:T(8,128)S(1)}, u32[]{:S(2)}, u32[]{:S(2)}) %collective-permute-start.1) | collective-permute-done | bytes 2097184 | tf_op jit(solution)/shard_map/ppermute | solution.py:65
  414.5 5.7 %fusion.80 = (f32[]{:T(128)}, f32[256,16,128]{2,0,1:T(8,128)S(1)}, f32[256,16,128]{2,0,1:T(8,128)}) fusion(f32[256,16,128]{2,0,1:T(8,128)S(1)} %fusion.56, f32[256,16,128]{2,0,1:T(8,128)S(1)} %fusion.47, f32[256,16,128]{2,0,1:T(8,128)S(1)} %fusion.53, f32[256,16,128]{2,0,1:T(8,128)S(1)} %fusion.30, f32[256,16,128]{2,1,0:T(8,128)S(1)} %get-tuple-element.32), kind=kOutput, calls=%fused_computation.115 | convolution fusion | flops 811302912 | bytes 14680068 | tf_op jit(solution)/shard_map/man,nk->mak/dot_general | solution.py:69
  423.4 3.2 fusion.14
  426.5 3.2 fusion.16
  429.8 3.4 fusion.62
  433.1 3.2 fusion.59
  445.3 3.3 fusion.7
  448.6 4.8 %fusion.1 = f32[1,256,2048]{2,1,0:T(8,128)} fusion(f32[256,2048]{1,0:T(8,128)S(1)} %fusion.7, f32[32,8,16,128]{3,2,1,0:T(8,128)S(1)} %bitcast.231), kind=kOutput, calls=%fused_computation.8 | convolution fusion | flops 1612578816 | bytes 6291456 | tf_op jit(solution)/shard_map/ab,bc->ac/dot_general | solution.py:69
  (112 shorter events, 113.0 us)
Async XLA Ops:
  7.2 128.2 %reduce-scatter.2.cloned.1.call-start = ((), (), s32[]{:S(2)}) async-start(), calls=%async_computation.2 | async-start | bytes 5406720 | tf_op jit(solution)/shard_map/reduce_scatter | solution.py:27
  31.2 205.1 %all-gather.3.cloned.1.call-start = ((), (), s32[]{:S(2)}) async-start(), calls=%async_computation.3 | async-start | bytes 8650752 | tf_op jit(solution)/shard_map/all_gather | solution.py:55
  136.4 33.8 %slice-start = ((s8[5242880]{0:T(1024)(128)(4,1)}), s8[1048576]{0:T(1024)(128)(4,1)S(1)}, s32[]{:S(2)}) async-start(s8[5242880]{0:T(1024)(128)(4,1)} %bitcast.218), calls=%async_computation.4 | async-start | bytes 2097152
  158.5 1.8 copy-start.7
  163.5 6.7 %slice-start.1 = ((s8[5242880]{0:T(1024)(128)(4,1)}), s8[4194304]{0:T(1024)(128)(4,1)S(1)}, s32[]{:S(2)}) async-start(s8[5242880]{0:T(1024)(128)(4,1)} %bitcast.218), calls=%async_computation.5 | async-start | bytes 8388608
  242.4 3.3 copy-start.5
  245.7 6.8 %copy-start.2 = (f32[256,2048]{1,0:T(8,128)S(1)}, f32[256,2048]{1,0:T(8,128)}, u32[]{:S(2)}) copy-start(f32[256,2048]{1,0:T(8,128)} %slice_reduce_fusion) | copy-start | bytes 6291460
  252.5 8.8 %slice-start.2 = ((s8[5242880]{0:T(1024)(128)(4,1)}), s8[4194304]{0:T(1024)(128)(4,1)S(1)}, s32[]{:S(2)}) async-start(s8[5242880]{0:T(1024)(128)(4,1)} %bitcast.221), calls=%async_computation.6 | async-start | bytes 8388608
  256.9 4.4 slice-start.3
  267.0 7.2 %copy-start.6 = (f32[320,256]{1,0:T(8,128)S(1)}, f32[320,256]{1,0:T(8,128)}, u32[]{:S(2)}) copy-start(f32[320,256]{1,0:T(8,128)} %get-tuple-element.11) | copy-start | bytes 983044
  267.0 9.5 %copy-start.4 = (f32[32,8,16,128]{3,1,2,0:T(8,128)S(1)}, f32[32,8,16,128]{3,1,2,0:T(8,128)}, u32[]{:S(2)}) copy-start(f32[32,8,16,128]{3,1,2,0:T(8,128)} %fusion.65) | copy-start | bytes 6291460
  274.2 2.6 copy-start.3
  274.3 17.2 %collective-permute-start = (f32[320,256]{1,0:T(8,128)S(1)}, f32[320,256]{1,0:T(8,128)S(1)}, u32[]{:S(2)}, u32[]{:S(2)}) collective-permute-start(f32[320,256]{1,0:T(8,128)S(1)} %copy-done.6), channel_id=1, source_target_pairs={{1,0},{2,1},{3,2},{4,3},{5,4},{6,5},{7,6},{8,7},{9,8},{10,9},{11,1... | collective-permute-start | bytes 983048 | tf_op jit(solution)/shard_map/ppermute | solution.py:65
  284.6 95.8 %collective-permute-start.1 = (f32[256,2048]{1,0:T(8,128)}, f32[256,2048]{1,0:T(8,128)S(1)}, u32[]{:S(2)}, u32[]{:S(2)}) collective-permute-start(f32[256,2048]{1,0:T(8,128)} %dynamic-slice_divide_fusion), channel_id=1, source_target_pairs={{0,8},{1,9},{2,10},{3,11},{4,12},{5,13},{6,14},{7,15},{8,16},{9,17... | collective-permute-start | bytes 6291464 | tf_op jit(solution)/shard_map/ppermute | solution.py:65
  296.7 4.0 copy-start.8
  296.9 3.9 copy-start.9
  390.9 2.3 copy-start
  390.9 2.3 copy-start.1
Sparse Core Ops, SparseCore 0:
  31.3 104.0 reduce-scatter.1
  160.4 75.7 all-gather.2
where the time goes:
time: 466 us; the launch traced here: 461 us
  waiting for transfers between devices  224 us (48%)
  matrix products  133 us (29%)
  other arithmetic  35.4 us (8%)
  local copies, waits for them, and re-layouts  22.5 us (5%)
  blocking collectives  21.5 us (5%)
  between operations  19.1 us (4%)
  starting transfers between devices  5.84 us (1%)
    dot_general x60, matrix products, contract(): return jnp.einsum(pattern, left, right, precision=HIGHEST)  133 us
    reduce_scatter x1, waiting for transfers between devices, one_scatter(): lax.psum_scatter(lines, axis, tiled=True).reshape(-1)  104 us
    all_gather x1, waiting for transfers between devices, sent_together(): out, at, outs = (lax.all_gather(both, axis, axis=dim, tiled=True), 0, [])  64.3 us
    ppermute x2, waiting for transfers between devices, shifted(): lax.ppermute(value, axis, [(source, source + steps) for source in range(f...  55.1 us
    all_to_all x1, blocking collectives, copy_for_each(): return lax.all_to_all(copies, axis, split_axis=0, concat_axis=0, tiled=True)  21.5 us
  transfers between devices with their start and end apart: 4, of which 3 were waited for; matrix products, arithmetic and copies ran while one was open for 12% of the time, Pallas kernels for 0%

commit v1 on v0

v1 whole, which is shorter than its diff:
```python
import math

import jax
import jax.numpy as jnp
import ml_dtypes
import numpy as np
from jax import lax
from jax.experimental import pallas as pl
from jax.experimental.pallas import tpu as pltpu
from jax.sharding import PartitionSpec as P

ROWS = 320
WIDTH = 2048
CUT = 256
GRID_COLS = 8
TILES = 256
PLANES = 2
HALF = 144
EAST_HALF = 176
MESH = pl.DeviceIdType.MESH
F32 = jnp.float32
BF16 = jnp.bfloat16


def two_parts(table):
    high = table.astype(ml_dtypes.bfloat16)
    low = (table - high.astype(np.float64)).astype(ml_dtypes.bfloat16)
    return high, low


def left_table(table):
    high, low = two_parts(table)
    return np.concatenate([high, high, low], axis=1)


def right_table(table):
    high, low = two_parts(table)
    return np.concatenate([high, high, low], axis=0)


def angles(rows, cols, length):
    product = np.outer(np.arange(rows), np.arange(cols)) % length
    return product * (2.0 * np.pi / length)


def row_tables(length, half, cols):
    count = length // 2 + 1
    turn = angles(count, length, length)
    forward = np.zeros((2 * half, length))
    forward[:count] = np.cos(turn)
    forward[half : half + count] = -np.sin(turn)
    weight = np.full((count, 1), 2.0)
    weight[0] = weight[-1] = 1.0
    scale = 1.0 / math.sqrt(length * cols)
    backward = np.zeros((length, 2 * half))
    backward[:, :count] = (weight * np.cos(turn)).T * scale
    backward[:, half : half + count] = (weight * np.sin(turn)).T * scale
    rows = np.zeros((half, 128), np.float32)
    rows[:count] = weight
    return left_table(forward), left_table(backward), rows


def south_tables():
    forward, backward, weight = row_tables(CUT, HALF, WIDTH)
    turn = angles(128, 128, 128)
    cos, sin = np.cos(turn), np.sin(turn)
    block = np.block([[cos, -sin], [sin, cos]])
    turn = angles(16, 128, WIDTH)
    twist = np.concatenate([np.cos(turn), -np.sin(turn)]).astype(np.float32)
    return forward, backward, weight, right_table(block), twist


def east_tables():
    forward, backward, weight = row_tables(ROWS, EAST_HALF, CUT)
    turn = angles(CUT, CUT, CUT)
    both = np.concatenate([np.cos(turn), np.sin(turn)], axis=1)
    return forward, backward, weight, right_table(both)


def dot(a, b):
    return jnp.dot(a, b, preferred_element_type=F32)


def three(x, axis):
    high = x.astype(BF16)
    low = (x - high.astype(F32)).astype(BF16)
    return jnp.concatenate([high, low, high], axis=axis)


def butterfly(re, im):
    size = len(re)
    if size == 1:
        return re, im
    even_re, even_im = butterfly(re[::2], im[::2])
    odd_re, odd_im = butterfly(re[1::2], im[1::2])
    top_re, top_im, low_re, low_im = [], [], [], []
    root = math.sqrt(0.5)
    for k in range(size // 2):
        a, b = odd_re[k], odd_im[k]
        if k == 0:
            pass
        elif 4 * k == size:
            a, b = b, -a
        elif 8 * k == size:
            a, b = root * (a + b), root * (b - a)
        elif 8 * k == 3 * size:
            a, b = root * (b - a), -root * (a + b)
        else:
            c, s = math.cos(2 * math.pi * k / size), math.sin(2 * math.pi * k / size)
            a, b = c * a + s * b, c * b - s * a
        top_re.append(even_re[k] + a)
        top_im.append(even_im[k] + b)
        low_re.append(even_re[k] - a)
        low_im.append(even_im[k] - b)
    return top_re + low_re, top_im + low_im


def at(start, size, step):
    return pl.ds(pl.multiple_of(start, step), size)


def loop(count, f):
    lax.fori_loop(0, count, lambda i, c: (f(i), c)[1], 0)


def south_forward(strip, dark, inv, rows3, cols3, twist, y, z, spec):
    def rows_step(i):
        cols = at(i * 256, 256, 256)
        x = (strip[:, cols] - dark[:, cols]) * inv[:, cols]
        y[:, cols] = dot(rows3[...], three(x, 0))

    loop(8, rows_step)

    def turn_step(i):
        top, low = at(i * 8, 8, 8), at(HALF + i * 8, 8, 8)
        re = [y[top, 128 * a : 128 * a + 128] for a in range(16)]
        im = [y[low, 128 * a : 128 * a + 128] for a in range(16)]
        re, im = butterfly(re, im)
        for k in range(16):
            c, s = twist[k : k + 1, :], twist[16 + k : 17 + k, :]
            to = at(k * HALF + i * 8, 8, 8)
            z[to, :128] = re[k] * c - im[k] * s
            z[to, 128:] = re[k] * s + im[k] * c

    loop(HALF // 8, turn_step)

    def cols_step(i):
        to = at(i * 576, 576, 8)
        spec[to, :] = dot(three(z[to, :], 1), cols3[...])

    loop(4, cols_step)


def own_kernel(strip, dark, inv, rows3, cols3, twist, spec, y, z):
    south_forward(strip, dark, inv, rows3, cols3, twist, y, z, spec)


def south_kernel(own, strip, dark, inv, rows3, back3, weight, cols3, twist, out, y, z, spec, mag):
    south_forward(strip, dark, inv, rows3, cols3, twist, y, z, spec)

    def cross_step(i, total):
        part = jnp.zeros((8, 128), F32)
        for k in range(16):
            here = at(k * HALF + i * 8, 8, 8)
            ar, ai = own[here, :128], own[here, 128:]
            br, bi = spec[here, :128], spec[here, 128:]
            cr = ar * br + ai * bi
            ci = ai * br - ar * bi
            size = jnp.sqrt(cr * cr + ci * ci)
            z[here, :128] = cr
            z[here, 128:] = -ci
            mag[here, :] = size
            part = part + size
        return total + part * weight[at(i * 8, 8, 8), :]

    total = lax.fori_loop(0, HALF // 8, cross_step, jnp.zeros((8, 128), F32))
    floor = jnp.sum(total) * (1.0 / (CUT * WIDTH)) + 1e-06

    def cols_step(i):
        here = at(i * 288, 288, 8)
        scale = 1.0 / (mag[here, :] + floor)
        x = jnp.concatenate([z[here, :128] * scale, z[here, 128:] * scale], axis=1)
        spec[here, :] = dot(three(x, 1), cols3[...])

    loop(8, cols_step)

    def turn_step(i):
        re, im = [], []
        for k in range(16):
            c, s = twist[k : k + 1, :], twist[16 + k : 17 + k, :]
            here = at(k * HALF + i * 8, 8, 8)
            a, b = spec[here, :128], spec[here, 128:]
            re.append(a * c - b * s)
            im.append(a * s + b * c)
        re, im = butterfly(re, im)
        top, low = at(i * 8, 8, 8), at(HALF + i * 8, 8, 8)
        for a in range(16):
            y[top, 128 * a : 128 * a + 128] = re[a]
            y[low, 128 * a : 128 * a + 128] = im[a]

    loop(HALF // 8, turn_step)

    def rows_step(i):
        cols = at(i * 256, 256, 256)
        out[:, cols] = dot(back3[...], three(y[:, cols], 0))

    loop(8, rows_step)


def east_kernel(own, other, dark, inv, dark2, inv2, rows3, back3, weight, cols3, out):
    half = EAST_HALF
    x = jnp.concatenate([(own[...] - dark[...]) * inv[...], (other[...] - dark2[...]) * inv2[...]], axis=1)
    y = dot(rows3[...], three(x, 0))

    def columns(v):
        p = dot(three(v, 1), cols3[...])
        return p[:half, :CUT] + p[half:, CUT:], p[half:, :CUT] - p[:half, CUT:]

    ar, ai = columns(y[:, :CUT])
    br, bi = columns(y[:, CUT:])
    cr = ar * br + ai * bi
    ci = ai * br - ar * bi
    size = jnp.sqrt(cr * cr + ci * ci)
    weighted = (size[:, :128] + size[:, 128:]) * weight[...]
    floor = jnp.sum(weighted) * (1.0 / (ROWS * CUT)) + 1e-06
    scale = 1.0 / (size + floor)
    vr, vi = columns(jnp.concatenate([cr * scale, -ci * scale], axis=0))
    out[...] = dot(back3[...], three(jnp.concatenate([vr, vi], axis=0), 0))


def log_kernel(raw, out):
    first, second = jnp.log(raw[0]), jnp.log(raw[1])
    out[0] = first + second
    out[1] = jnp.minimum(first, second)


def logs_of(tile):
    rows = 32
    return pl.pallas_call(
        log_kernel,
        grid=(ROWS // rows,),
        in_specs=[pl.BlockSpec((PLANES, rows, WIDTH), lambda i: (0, i, 0))],
        out_specs=pl.BlockSpec((2, rows, WIDTH), lambda i: (0, i, 0)),
        out_shape=jax.ShapeDtypeStruct((2, ROWS, WIDTH), F32),
        cost_estimate=pl.CostEstimate(flops=4 * ROWS * WIDTH, bytes_accessed=16 * ROWS * WIDTH, transcendentals=2 * ROWS * WIDTH),
        name="logs",
    )(tile)


SIDE = ROWS // 2


def field_kernel(logs, out, acc, first, recv1, recv2, recv3, recv4, recv_z, recv_a, recv_b, send, recv):
    gz, ta = lax.axis_index("gz"), lax.axis_index("ta")
    y, z_lo = gz // 2, gz % 2
    z_hi, x, core = ta // 8, (ta // 2) % 4, ta % 2

    def device(x, y, z_hi, z_lo, core):
        return (y * 2 + z_lo, z_hi * 8 + x * 2 + core)

    def beside(p):
        return p + 1 - 2 * (p % 2)

    def across(p):
        return 3 - p

    def gray(p):
        return (p + p // 2) % 2

    other = 1 - core

    def along(axis, move):
        on_x = (1 - core) if axis == 0 else core
        return device(x + on_x * (move(x) - x), y + (1 - on_x) * (move(y) - y), z_hi, z_lo, core)

    place = (x + core * (y - x), y + core * (x - y))
    partner_core = device(x, y, z_hi, z_lo, other)
    partner = {(axis, move): along(axis, move) for axis in (0, 1) for move in (beside, across)}
    partner_lo = device(x, y, z_hi, 1 - z_lo, core)
    partner_a = device(x, y, beside(z_hi), z_lo, core)
    partner_b = device(x, y, across(z_hi), z_lo, core)

    barrier = pltpu.get_barrier_semaphore()
    everyone = [partner_core, *partner.values(), partner_lo, partner_a, partner_b]
    for d in everyone:
        pl.semaphore_signal(barrier, inc=1, device_id=d, device_id_type=MESH)
    pl.semaphore_wait(barrier, len(everyone))

    count = [0]
    started = []

    def copy(src, dst, to):
        i = count[0]
        count[0] += 1
        c = pltpu.make_async_remote_copy(
            src_ref=src, dst_ref=dst, send_sem=send.at[i], recv_sem=recv.at[i], device_id=to, device_id_type=MESH
        )
        c.start()
        started.append(c)
        return c

    def rows(k):
        return pl.ds(k * SIDE, SIDE)

    flight = [copy(logs.at[other, rows(k)], first.at[rows(k)], partner_core) for k in (0, 1)]
    moves = [
        [(0, beside, gray), (0, across, lambda p: p // 2), (1, beside, gray), (1, across, lambda p: p // 2)],
        [(0, across, lambda p: p // 2), (0, beside, gray), (1, across, lambda p: p // 2), (1, beside, gray)],
    ]
    into = [recv1, recv2, recv3, recv4]
    widths = [1024, 512, 256, 128]
    bases = [[0], [0]]
    bits = [[], []]
    for step in range(5):
        for k in (0, 1):
            flight[k].wait_recv()
            if step == 0:

                def add_first(i, k=k):
                    r = at(k * SIDE + i * 8, 8, 8)
                    acc[r, :] = logs[core, r, :] + first[r, :]

                loop(SIDE // 8, add_first)
            else:
                w = widths[step - 1]
                base = bases[k][step]
                buf = into[step - 1]

                def add_next(i, k=k, w=w, base=base, buf=buf):
                    r = at(k * SIDE + i * 8, 8, 8)
                    c = at(base, w, 128)
                    acc[r, c] = acc[r, c] + buf[k, at(i * 8, 8, 8), :]

                loop(SIDE // 8, add_next)
            if step < 4:
                axis, move, bit = moves[k][step]
                w = widths[step]
                b = bit(place[axis])
                base = bases[k][step]
                flight[k] = copy(
                    acc.at[rows(k), at(base + (1 - b) * w, w, 128)], into[step].at[k], partner[(axis, move)]
                )
                bases[k].append(base + b * w)
                bits[k].append(b)

    col_a, col_b = bases[0][4], bases[1][4]
    mine = col_a + z_lo * (col_b - col_a)
    theirs = col_b + z_lo * (col_a - col_b)
    col = at(mine, 128, 128)
    top = z_lo * SIDE
    f = copy(acc.at[at((1 - z_lo) * SIDE, SIDE, 8), at(theirs, 128, 128)], recv_z, partner_lo)
    f.wait_recv()
    acc[at(top, SIDE, 8), col] += recv_z[...]
    g, h = gray(z_hi), z_hi // 2
    f = copy(acc.at[at(top + (1 - g) * 80, 80, 8), col], recv_a, partner_a)
    top_a = top + g * 80
    f.wait_recv()
    acc[at(top_a, 80, 8), col] += recv_a[...]
    f = copy(acc.at[at(top_a + (1 - h) * 40, 40, 8), col], recv_b, partner_b)
    top_b = top_a + h * 40
    f.wait_recv()
    total = acc[at(top_b, 40, 8), col] + recv_b[...]
    is_floor = core.astype(F32)
    scale = is_floor * (1.0 / TILES) - (1.0 - is_floor) * (1.0 / (TILES * PLANES))
    out[core, at(top_b, 40, 8), col] = (1.0 - 0.5 * is_floor) * jnp.exp(total * scale)

    def give(r, c, to):
        return copy(out.at[core, r, c], out.at[core, r, c], to)

    give(at(top_b, 40, 8), col, partner_b).wait_recv()
    give(at(top_a, 80, 8), col, partner_a).wait_recv()
    give(at(top, SIDE, 8), col, partner_lo).wait_recv()
    for step in (3, 2, 1, 0):
        for k in (0, 1):
            if step < 3:
                flight[k].wait_recv()
            axis, move, _ = moves[k][step]
            w = widths[step]
            flight[k] = give(rows(k), at(bases[k][step + 1], w, 128), partner[(axis, move)])
    for k in (0, 1):
        flight[k].wait_recv()
        flight[k] = copy(out.at[core, rows(k)], out.at[core, rows(k)], partner_core)
    for k in (0, 1):
        flight[k].wait_recv()
    for c in started:
        c.wait_send()


COPIES = 2 + 8 + 3 + 3 + 8 + 2


def fields_of(logs):
    return pl.pallas_call(
        field_kernel,
        out_shape=jax.ShapeDtypeStruct((2, ROWS, WIDTH), F32),
        in_specs=[pl.BlockSpec(memory_space=pltpu.VMEM)],
        out_specs=pl.BlockSpec(memory_space=pltpu.VMEM),
        scratch_shapes=[
            pltpu.VMEM((ROWS, WIDTH), F32),
            pltpu.VMEM((ROWS, WIDTH), F32),
            pltpu.VMEM((2, SIDE, 1024), F32),
            pltpu.VMEM((2, SIDE, 512), F32),
            pltpu.VMEM((2, SIDE, 256), F32),
            pltpu.VMEM((2, SIDE, 128), F32),
            pltpu.VMEM((SIDE, 128), F32),
            pltpu.VMEM((80, 128), F32),
            pltpu.VMEM((40, 128), F32),
            pltpu.SemaphoreType.DMA((COPIES,)),
            pltpu.SemaphoreType.DMA((COPIES,)),
        ],
        compiler_params=pltpu.CompilerParams(collective_id=0, has_side_effects=True, vmem_limit_bytes=30 << 20),
        cost_estimate=pl.CostEstimate(flops=8 * ROWS * WIDTH, bytes_accessed=100 << 20, transcendentals=40 * 128),
        name="fields",
    )(logs)


def plain_call(kernel, out, scratch, flops, args, name):
    return pl.pallas_call(
        kernel,
        out_shape=jax.ShapeDtypeStruct(out, F32),
        scratch_shapes=[pltpu.VMEM(s, F32) for s in scratch],
        compiler_params=pltpu.CompilerParams(vmem_limit_bytes=40 << 20),
        cost_estimate=pl.CostEstimate(flops=flops, bytes_accessed=8 << 20, transcendentals=0),
        name=name,
    )(*args)


def shifted(value, steps, count):
    first, last = (max(0, -steps), min(count, count - steps))
    return lax.ppermute(value, "ta", [(source, source + steps) for source in range(first, last)])


def body(raw_planes, offsets):
    tile = raw_planes[0]
    count = lax.axis_size("ta")
    slot = lax.axis_index("ta")
    own_tile = lax.axis_index("gz") * count + slot
    has_east = slot < count - 1
    has_north = slot >= GRID_COLS
    own_east = offsets[own_tile, 0]
    own_south = offsets[own_tile, 1]
    north_south = offsets[jnp.maximum(own_tile - GRID_COLS, 0), 1]

    south_mean = jnp.mean(lax.dynamic_slice_in_dim(tile, ROWS - CUT - own_south, CUT, 1), 0)
    south_in = shifted(south_mean, GRID_COLS, count)
    west_in = shifted(jnp.mean(tile[:, :, :CUT], 0), -1, count)

    fields = fields_of(logs_of(tile))
    inv, dark = fields[0], fields[1]
    corrected = (tile - dark) * inv

    east_start = WIDTH - CUT - own_east
    east_mean = jnp.mean(lax.dynamic_slice_in_dim(tile, east_start, CUT, 2), 0)
    east_dark = lax.dynamic_slice_in_dim(dark, east_start, CUT, 1)
    east_inv = lax.dynamic_slice_in_dim(inv, east_start, CUT, 1)
    west_inv = jnp.where(has_east, inv[:, :CUT], 0.0)
    forward, backward, weight, cols3 = east_tables()
    east_corr = plain_call(
        east_kernel,
        (ROWS, CUT),
        [],
        10**9,
        (east_mean, west_in, east_dark, east_inv, dark[:, :CUT], west_inv, forward, backward, weight, cols3),
        "east",
    )

    forward, backward, weight, cols3, twist = south_tables()
    north_mean = jnp.mean(tile[:, :CUT], 0)
    own_spec = plain_call(
        own_kernel,
        (16 * HALF, 256),
        [(2 * HALF, WIDTH), (16 * HALF, 256)],
        2 * 10**9,
        (north_mean, dark[:CUT], inv[:CUT], forward, cols3, twist),
        "own",
    )
    start = ROWS - CUT - north_south
    south_dark = lax.dynamic_slice_in_dim(dark, start, CUT, 0)
    south_inv = jnp.where(has_north, lax.dynamic_slice_in_dim(inv, start, CUT, 0), 0.0)
    south_corr = plain_call(
        south_kernel,
        (CUT, WIDTH),
        [(2 * HALF, WIDTH), (16 * HALF, 256), (16 * HALF, 256), (16 * HALF, 128)],
        4 * 10**9,
        (own_spec, south_in, south_dark, south_inv, forward, backward, weight, cols3, twist),
        "south",
    )
    return (corrected[None], east_corr[None], south_corr[None])


def solution(mesh):
    in_specs = (P(("gz", "ta"), None, None, None), P())
    out_specs = (
        P(("gz", "ta"), None, None, None),
        P(("gz", "ta"), None, None),
        P(("gz", "ta"), None, None),
    )
    return jax.shard_map(body, mesh=mesh, in_specs=in_specs, out_specs=out_specs, check_vma=False)
```

time: 466 us -> 213 us (0.46)
  the two profiles are of different devices: /device:TPU:98 before, /device:TPU:1 now
where the time goes in v1:
time: 213 us; the launch traced here: 210 us
  Pallas kernels  163 us (77%)
  other arithmetic  16.9 us (8%)
  local copies, waits for them, and re-layouts  15.9 us (7%)
  starting transfers between devices  9.58 us (4%)
  between operations  4.83 us (2%)
    pallas_call x1, Pallas kernels, fields_of(): pl.pallas_call(field_kernel, out_shape=jax.ShapeDtypeStruct((2, ROWS, WID...  131 us
    pallas_call x3, Pallas kernels, plain_call(): pl.pallas_call(kernel, out_shape=jax.ShapeDtypeStruct(out, F32), scratch_...  23.8 us
    ppermute x2, starting transfers between devices, shifted(): lax.ppermute(value, 'ta', [(source, source + steps) for source in range(f...  9.58 us
    pallas_call x1, Pallas kernels, logs_of(): pl.pallas_call(log_kernel, grid=(ROWS // rows,), in_specs=[pl.BlockSpec((...  8.11 us
    mul x1, other arithmetic, body(): corrected = (tile - dark) * inv  6.11 us
    unnamed x38, local copies, waits for them, and re-layouts  5.13 us
    slice x1, local copies, waits for them, and re-layouts, body(): inv, dark = (fields[0], fields[1])  4.67 us
  transfers between devices with their start and end apart: 2, of which 0 were waited for; matrix products, arithmetic and copies ran while one was open for 12% of the time, Pallas kernels for 71%

profile of v1, /device:TPU:1, one launch (start us, length us, event | category | flops | bytes accessed | tf_op | source)
XLA Modules:
  0.0 209.8 jit_solution(14674565196878855343)
XLA Ops:
  0.6 1.2 slice_reduce_fusion.1
  1.8 0.7 broadcast_multiply_fusion.2
  2.6 5.1 %collective-permute-start = (f32[320,256]{1,0:T(8,128)}, f32[320,256]{1,0:T(8,128)}, u32[]{:S(2)}, u32[]{:S(2)}) collective-permute-start(f32[320,256]{1,0:T(8,128)} %broadcast_multiply_fusion.2), channel_id=1, source_target_pairs={{1,0},{2,1},{3,2},{4,3},{5,4},{6,5},{7,6},{8,7},{9,8},{10,9},{11,1... | collective-permute-start | bytes 983048 | tf_op jit(solution)/shard_map/ppermute | solution.py:430
  7.7 1.5 constant_dynamic-slice_fusion.1
  10.5 3.2 %dynamic-slice_reduce_fusion = f32[256,2048]{1,0:T(8,128)S(1)} fusion(f32[1,2,320,2048]{3,2,1,0:T(8,128)} %param.11, s32[]{:T(128)S(6)} %select_n.39), kind=kLoop, calls=%fused_computation.2 | loop fusion | flops 524288 | bytes 6291460 | tf_op jit(solution)/shard_map/reduce_sum | solution.py:444
  13.6 1.5 broadcast_multiply_fusion
  15.2 4.5 %collective-permute-start.1 = (f32[256,2048]{1,0:T(8,128)}, f32[256,2048]{1,0:T(8,128)}, u32[]{:S(2)}, u32[]{:S(2)}) collective-permute-start(f32[256,2048]{1,0:T(8,128)} %broadcast_multiply_fusion), channel_id=1, source_target_pairs={{0,8},{1,9},{2,10},{3,11},{4,12},{5,13},{6,14},{7,15},{8,16},{9,17... | collective-permute-start | bytes 6291464 | tf_op jit(solution)/shard_map/ppermute | solution.py:430
  19.7 1.7 slice_reduce_fusion
  21.4 8.1 %logs.1 = f32[2,320,2048]{2,1,0:T(8,128)} custom-call(f32[2,320,2048]{2,1,0:T(8,128)} %bitcast.26), custom_call_target="tpu_custom_call" | custom-call | flops 2621440 | bytes 10485760 | tf_op jit(solution)/shard_map/logs/pallas_call | solution.py:239
  29.5 2.5 %copy-done = f32[2,320,2048]{2,1,0:T(8,128)S(1)} copy-done((f32[2,320,2048]{2,1,0:T(8,128)S(1)}, f32[2,320,2048]{2,1,0:T(8,128)}, u32[]{:S(2)}) %copy-start) | copy-done | bytes 5242904
  32.0 130.8 %fields.1 = f32[2,320,2048]{2,1,0:T(8,128)S(1)} custom-call(f32[2,320,2048]{2,1,0:T(8,128)S(1)} %copy-done), custom_call_target="tpu_custom_call" | custom-call | flops 5242880 | bytes 104857600 | tf_op jit(solution)/shard_map/fields/pallas_call | solution.py:393
  162.8 2.2 %slice_bitcast_fusion = (f32[256,2048]{1,0:T(8,128)}, f32[256,2048]{1,0:T(8,128)}) fusion(f32[2,320,2048]{2,1,0:T(8,128)S(1)} %fields.1), kind=kLoop, calls=%fused_computation.5 | loop fusion | bytes 8388608 | tf_op jit(solution)/shard_map/slice | solution.py:474
  165.0 4.7 %fusion = (f32[1,320,2048]{2,1,0:T(8,128)}, f32[320,2048]{1,0:T(8,128)}, f32[320,2048]{1,0:T(8,128)}, f32[1,320,2048]{2,1,0:T(8,128)}) fusion(f32[2,320,2048]{2,1,0:T(8,128)S(1)} %fields.1), kind=kLoop, calls=%fused_computation.21 | loop fusion | bytes 15728640 | tf_op jit(solution)/shard_map/slice | solution.py:449
  169.7 0.2 broadcast_multiply_fusion.1.strip
  172.5 1.0 slice.43.dark2
  173.6 1.6 dynamic-slice_reduce_fusion.1
  175.2 1.4 dynamic-slice_bitcast_fusion.1
  176.6 1.6 copy-done.2
  178.2 4.9 %own.1 = f32[2304,256]{1,0:T(8,128)S(1)} custom-call(f32[256,2048]{1,0:T(8,128)S(1)} %broadcast_multiply_fusion.1.strip, f32[256,2048]{1,0:T(8,128)S(1)} %copy-done.2, f32[256,2048]{1,0:T(8,128)S(1)} %copy-done.1, bf16[288,768]{1,0:T(8,128)(2,1)S(1)} %copy-done.6, bf16[768,256]{1,0:T(8,128)(2,1)S(1)} %copy-done.7, f32[32,128]{1,0:T(8,128)S(1)} %copy-done.9), custom_call_target="tpu_custom_call" | custom-call | flops 2000000000 | bytes 8388608 | tf_op jit(solution)/shard_map/own/pallas_call | solution.py:418
  183.2 6.1 %subtract_multiply_fusion = f32[1,2,320,2048]{3,2,1,0:T(8,128)} fusion(f32[1,2,320,2048]{3,2,1,0:T(8,128)} %param.11, f32[320,2048]{1,0:T(8,128)S(1)} %copy-done.13, f32[320,2048]{1,0:T(8,128)S(1)} %copy-done.12), kind=kLoop, calls=%fused_computation | loop fusion | flops 2621440 | bytes 15728640 | tf_op jit(solution)/shard_map/mul | solution.py:450
  189.4 0.5 select_bitcast_fusion
  189.9 0.5 copy-done.3
  190.9 4.4 %east.1 = f32[320,256]{1,0:T(8,128)} custom-call(f32[320,256]{1,0:T(8,128)S(1)} %broadcast_multiply_fusion.3.own, f32[320,256]{1,0:T(8,128)} %collective-permute-done.other, f32[320,256]{1,0:T(8,128)S(1)} %get-tuple-element.15.dark, f32[320,256]{1,0:T(8,128)S(1)} %get-tuple-element.14.inv, f32[320,256]{1,0:T(8,128)S(1)} %slice.43.dark2, ...), custom_call_target="tpu_custom_call" | custom-call | flops 1000000000 | bytes 8388608 | tf_op jit(solution)/shard_map/east/pallas_call | solution.py:418
  195.3 14.5 %south.1 = f32[256,2048]{1,0:T(8,128)} custom-call(f32[2304,256]{1,0:T(8,128)S(1)} %own.1, f32[256,2048]{1,0:T(8,128)} %collective-permute-done.1.strip, f32[256,2048]{1,0:T(8,128)S(1)} %get-tuple-element.13.dark, f32[256,2048]{1,0:T(8,128)S(1)} %get-tuple-element.12.inv, bf16[288,768]{1,0:T(8,128)(2,1)S(1)} %copy-done.6, bf16[256,864]{1,0:T(8,128)(2,1)S(1)} %copy-done.10, ...), custom_call_target="tpu_custom_call" | custom-call | flops 4000000000 | bytes 8388608 | tf_op jit(solution)/shard_map/south/pallas_call | solution.py:418
  (40 shorter events, 0.6 us)
Async XLA Ops:
  2.6 187.4 %collective-permute-start = (f32[320,256]{1,0:T(8,128)}, f32[320,256]{1,0:T(8,128)}, u32[]{:S(2)}, u32[]{:S(2)}) collective-permute-start(f32[320,256]{1,0:T(8,128)} %broadcast_multiply_fusion.2), channel_id=1, source_target_pairs={{1,0},{2,1},{3,2},{4,3},{5,4},{6,5},{7,6},{8,7},{9,8},{10,9},{11,1... | collective-permute-start | bytes 983048 | tf_op jit(solution)/shard_map/ppermute | solution.py:430
  10.4 9.2 %slice-start = ((s8[5242880]{0:T(1024)(128)(4,1)}), s8[1048576]{0:T(1024)(128)(4,1)S(1)}, s32[]{:S(2)}) async-start(s8[5242880]{0:T(1024)(128)(4,1)} %bitcast.27), calls=%async_computation | async-start | bytes 2097152
  10.4 9.2 %slice-start.1 = ((s8[5242880]{0:T(1024)(128)(4,1)}), s8[4194304]{0:T(1024)(128)(4,1)S(1)}, s32[]{:S(2)}) async-start(s8[5242880]{0:T(1024)(128)(4,1)} %bitcast.27), calls=%async_computation.1 | async-start | bytes 8388608
  15.2 180.1 %collective-permute-start.1 = (f32[256,2048]{1,0:T(8,128)}, f32[256,2048]{1,0:T(8,128)}, u32[]{:S(2)}, u32[]{:S(2)}) collective-permute-start(f32[256,2048]{1,0:T(8,128)} %broadcast_multiply_fusion), channel_id=1, source_target_pairs={{0,8},{1,9},{2,10},{3,11},{4,12},{5,13},{6,14},{7,15},{8,16},{9,17... | collective-permute-start | bytes 6291464 | tf_op jit(solution)/shard_map/ppermute | solution.py:430
  29.5 2.5 %copy-start = (f32[2,320,2048]{2,1,0:T(8,128)S(1)}, f32[2,320,2048]{2,1,0:T(8,128)}, u32[]{:S(2)}) copy-start(f32[2,320,2048]{2,1,0:T(8,128)} %logs.1) | copy-start | bytes 15728644
  165.0 4.7 %copy-start.16 = (f32[256,2048]{1,0:T(8,128)S(1)}, f32[256,2048]{1,0:T(8,128)}, u32[]{:S(2)}) copy-start(f32[256,2048]{1,0:T(8,128)} %slice_reduce_fusion) | copy-start | bytes 6291460
  169.6 7.0 %copy-start.6 = (bf16[288,768]{1,0:T(8,128)(2,1)S(1)}, bf16[288,768]{1,0:T(8,128)(2,1)}, u32[]{:S(2)}) copy-start(bf16[288,768]{1,0:T(8,128)(2,1)} %constant.78.clone.rows3) | copy-start | bytes 1327108
  169.6 7.0 %copy-start.7 = (bf16[768,256]{1,0:T(8,128)(2,1)S(1)}, bf16[768,256]{1,0:T(8,128)(2,1)}, u32[]{:S(2)}) copy-start(bf16[768,256]{1,0:T(8,128)(2,1)} %constant.79.clone.cols3) | copy-start | bytes 1179652
  169.6 7.0 %copy-start.9 = (f32[32,128]{1,0:T(8,128)S(1)}, f32[32,128]{1,0:T(8,128)}, u32[]{:S(2)}) copy-start(f32[32,128]{1,0:T(8,128)} %constant.80.clone.twist) | copy-start | bytes 49156
  173.5 3.1 %copy-start.1 = (f32[256,2048]{1,0:T(8,128)S(1)}, f32[256,2048]{1,0:T(8,128)}, u32[]{:S(2)}) copy-start(f32[256,2048]{1,0:T(8,128)} %get-tuple-element.3.inv) | copy-start | bytes 6291460
  176.6 1.6 copy-start.2
  178.2 4.9 %copy-start.13 = (f32[320,2048]{1,0:T(8,128)S(1)}, f32[320,2048]{1,0:T(8,128)}, u32[]{:S(2)}) copy-start(f32[320,2048]{1,0:T(8,128)} %get-tuple-element.7) | copy-start | bytes 7864324
  178.2 5.0 %copy-start.12 = (f32[320,2048]{1,0:T(8,128)S(1)}, f32[320,2048]{1,0:T(8,128)}, u32[]{:S(2)}) copy-start(f32[320,2048]{1,0:T(8,128)} %get-tuple-element.6) | copy-start | bytes 7864324
  183.2 6.1 %copy-start.14 = (f32[1,320,2048]{2,1,0:T(8,128)S(1)}, f32[1,320,2048]{2,1,0:T(8,128)}, u32[]{:S(2)}) copy-start(f32[1,320,2048]{2,1,0:T(8,128)} %get-tuple-element.5) | copy-start | bytes 7864324
  183.2 6.1 %copy-start.15 = (f32[1,320,2048]{2,1,0:T(8,128)S(1)}, f32[1,320,2048]{2,1,0:T(8,128)}, u32[]{:S(2)}) copy-start(f32[1,320,2048]{2,1,0:T(8,128)} %get-tuple-element.8) | copy-start | bytes 7864324
  189.3 1.1 copy-start.3
  189.3 1.4 copy-start.4
  189.4 1.6 copy-start.5
  189.4 1.6 copy-start.8
  189.9 5.4 %copy-start.10 = (bf16[256,864]{1,0:T(8,128)(2,1)S(1)}, bf16[256,864]{1,0:T(8,128)(2,1)}, u32[]{:S(2)}) copy-start(bf16[256,864]{1,0:T(8,128)(2,1)} %constant.81.clone.back3) | copy-start | bytes 1327108
  189.9 5.4 %copy-start.11 = (f32[144,128]{1,0:T(8,128)S(1)}, f32[144,128]{1,0:T(8,128)}, u32[]{:S(2)}) copy-start(f32[144,128]{1,0:T(8,128)} %constant.82.clone.weight) | copy-start | bytes 221188

commit v2 on v1

v2 whole, which is shorter than its diff:
```python
import math

import jax
import jax.numpy as jnp
import ml_dtypes
import numpy as np
from jax import lax
from jax.experimental import pallas as pl
from jax.experimental.pallas import tpu as pltpu
from jax.sharding import PartitionSpec as P

ROWS = 320
WIDTH = 2048
CUT = 256
GRID_COLS = 8
TILES = 256
PLANES = 2
HALF = 144
EAST_HALF = 176
MESH = pl.DeviceIdType.MESH
F32 = jnp.float32
BF16 = jnp.bfloat16


def two_parts(table):
    high = table.astype(ml_dtypes.bfloat16)
    low = (table - high.astype(np.float64)).astype(ml_dtypes.bfloat16)
    return high, low


def stacked(table):
    return np.stack(two_parts(table))


def left_table(table):
    high, low = two_parts(table)
    return np.concatenate([high, high, low], axis=1)


def right_table(table):
    high, low = two_parts(table)
    return np.concatenate([high, high, low], axis=0)


def angles(rows, cols, length):
    product = np.outer(np.arange(rows), np.arange(cols)) % length
    return product * (2.0 * np.pi / length)


def row_tables(length, half, cols, left_table):
    count = length // 2 + 1
    turn = angles(count, length, length)
    forward = np.zeros((2 * half, length))
    forward[:count] = np.cos(turn)
    forward[half : half + count] = -np.sin(turn)
    weight = np.full((count, 1), 2.0)
    weight[0] = weight[-1] = 1.0
    scale = 1.0 / math.sqrt(length * cols)
    backward = np.zeros((length, 2 * half))
    backward[:, :count] = (weight * np.cos(turn)).T * scale
    backward[:, half : half + count] = (weight * np.sin(turn)).T * scale
    rows = np.zeros((half, 128), np.float32)
    rows[:count] = weight
    return left_table(forward), left_table(backward), rows


def south_tables():
    forward, backward, weight = row_tables(CUT, HALF, WIDTH, left_table)
    turn = angles(128, 128, 128)
    cos, sin = np.cos(turn), np.sin(turn)
    block = np.block([[cos, -sin], [sin, cos]])
    turn = angles(16, 128, WIDTH)
    twist = np.concatenate([np.cos(turn), -np.sin(turn)]).astype(np.float32)
    return forward, backward, weight, right_table(block), twist


def east_tables():
    forward, backward, weight = row_tables(ROWS, EAST_HALF, CUT, stacked)
    turn = angles(CUT, CUT, CUT)
    both = np.concatenate([np.cos(turn), np.sin(turn)], axis=1)
    return forward, backward, weight, stacked(both)


def dot(a, b):
    return jnp.dot(a, b, preferred_element_type=F32)


def three(x, axis):
    high, low = split(x)
    return jnp.concatenate([high, low, high], axis=axis)


def split(x):
    high = x.astype(BF16)
    return high, (x - high.astype(F32)).astype(BF16)


def left_dot(table, x):
    high, low = split(x)
    return dot(table[0], high) + (dot(table[0], low) + dot(table[1], high))


def right_dot(x, table):
    high, low = split(x)
    return dot(high, table[0]) + (dot(low, table[0]) + dot(high, table[1]))


def butterfly(re, im):
    size = len(re)
    if size == 1:
        return re, im
    even_re, even_im = butterfly(re[::2], im[::2])
    odd_re, odd_im = butterfly(re[1::2], im[1::2])
    top_re, top_im, low_re, low_im = [], [], [], []
    root = math.sqrt(0.5)
    for k in range(size // 2):
        a, b = odd_re[k], odd_im[k]
        if k == 0:
            pass
        elif 4 * k == size:
            a, b = b, -a
        elif 8 * k == size:
            a, b = root * (a + b), root * (b - a)
        elif 8 * k == 3 * size:
            a, b = root * (b - a), -root * (a + b)
        else:
            c, s = math.cos(2 * math.pi * k / size), math.sin(2 * math.pi * k / size)
            a, b = c * a + s * b, c * b - s * a
        top_re.append(even_re[k] + a)
        top_im.append(even_im[k] + b)
        low_re.append(even_re[k] - a)
        low_im.append(even_im[k] - b)
    return top_re + low_re, top_im + low_im


def at(start, size, step):
    return pl.ds(pl.multiple_of(start, step), size)


def loop(count, f):
    lax.fori_loop(0, count, lambda i, c: (f(i), c)[1], 0)


def moved(x, steps, axis):
    count = jnp.full(x.shape, steps, jnp.int32)
    for bit in (32, 16, 8, 4, 2, 1):
        x = jnp.where((count & bit) != 0, pltpu.roll(x, bit, axis), x)
    return x


def aligned(start):
    base = jnp.minimum(start // 8 * 8, ROWS - CUT - 8)
    return base, (16 - (start - base)) % 16


def south_forward(strip_of, rows3, cols3, twist, y, z, spec):
    def rows_step(i):
        cols = at(i * 256, 256, 256)
        y[:, cols] = dot(rows3[...], three(strip_of(cols), 0))

    loop(8, rows_step)

    def turn_step(i):
        top, low = at(i * 8, 8, 8), at(HALF + i * 8, 8, 8)
        re = [y[top, 128 * a : 128 * a + 128] for a in range(16)]
        im = [y[low, 128 * a : 128 * a + 128] for a in range(16)]
        re, im = butterfly(re, im)
        for k in range(16):
            c, s = twist[k : k + 1, :], twist[16 + k : 17 + k, :]
            to = at(k * HALF + i * 8, 8, 8)
            z[to, :128] = re[k] * c - im[k] * s
            z[to, 128:] = re[k] * s + im[k] * c

    loop(HALF // 8, turn_step)

    def cols_step(i):
        to = at(i * 576, 576, 8)
        spec[to, :] = dot(three(z[to, :], 1), cols3[...])

    loop(4, cols_step)


def south_kernel(
    offsets, own, tile, fields, strip, east, rows3, back3, weight, cols3, twist,
    corrected, east_out, out, y, z, spec, mag, ready, inv, dark, sems,
):
    slot = lax.axis_index("ta")
    north = jnp.maximum(lax.axis_index("gz") * lax.axis_size("ta") + slot - GRID_COLS, 0)
    start = ROWS - CUT - offsets[north, 1]
    has_north = (slot >= GRID_COLS).astype(F32)

    def correct(i):
        r = at(i * 8, 8, 8)
        for c in range(0, WIDTH, 512):
            cols = slice(c, c + 512)
            g, d = fields[0, r, cols], fields[1, r, cols]
            for p in range(PLANES):
                ready[p, r, cols] = (tile[p, r, cols] - d) * g

    loop(ROWS // 8, correct)
    writes = [pltpu.make_async_copy(ready, corrected, sems.at[0]), pltpu.make_async_copy(east, east_out, sems.at[1])]
    for w in writes:
        w.start()

    base, turn = aligned(start)

    def cut(i):
        for c in range(0, WIDTH, 512):
            cols = slice(c, c + 512)
            window = at(base + i * 8, 16, 8)
            inv[at(i * 8, 8, 8), cols] = pltpu.roll(fields[0, window, cols], turn, 0)[:8] * has_north
            dark[at(i * 8, 8, 8), cols] = pltpu.roll(fields[1, window, cols], turn, 0)[:8]

    loop(CUT // 8, cut)

    def strip_of(cols):
        return (0.5 * strip[:, cols] - dark[:, cols]) * inv[:, cols]

    south_forward(strip_of, rows3, cols3, twist, y, z, spec)

    def cross_step(i, total):
        part = jnp.zeros((8, 128), F32)
        for k in range(16):
            here = at(k * HALF + i * 8, 8, 8)
            ar, ai = own[here, :128], own[here, 128:]
            br, bi = spec[here, :128], spec[here, 128:]
            cr = ar * br + ai * bi
            ci = ai * br - ar * bi
            size = jnp.sqrt(cr * cr + ci * ci)
            z[here, :128] = cr
            z[here, 128:] = -ci
            mag[here, :] = size
            part = part + size
        return total + part * weight[at(i * 8, 8, 8), :]

    total = lax.fori_loop(0, HALF // 8, cross_step, jnp.zeros((8, 128), F32))
    floor = jnp.sum(total) * (1.0 / (CUT * WIDTH)) + 1e-06

    def cols_step(i):
        here = at(i * 288, 288, 8)
        scale = 1.0 / (mag[here, :] + floor)
        x = jnp.concatenate([z[here, :128] * scale, z[here, 128:] * scale], axis=1)
        spec[here, :] = dot(three(x, 1), cols3[...])

    loop(8, cols_step)

    def turn_step(i):
        re, im = [], []
        for k in range(16):
            c, s = twist[k : k + 1, :], twist[16 + k : 17 + k, :]
            here = at(k * HALF + i * 8, 8, 8)
            a, b = spec[here, :128], spec[here, 128:]
            re.append(a * c - b * s)
            im.append(a * s + b * c)
        re, im = butterfly(re, im)
        top, low = at(i * 8, 8, 8), at(HALF + i * 8, 8, 8)
        for a in range(16):
            y[top, 128 * a : 128 * a + 128] = re[a]
            y[low, 128 * a : 128 * a + 128] = im[a]

    loop(HALF // 8, turn_step)

    def rows_step(i):
        cols = at(i * 256, 256, 256)
        out[:, cols] = dot(back3[...], three(y[:, cols], 0))

    loop(8, rows_step)
    for w in writes:
        w.wait()


def east_into(out, x, rows3, back3, weight, cols3):
    half = EAST_HALF
    y = left_dot(rows3, x)

    def columns(v):
        p = right_dot(v, cols3)
        return p[:half, :CUT] + p[half:, CUT:], p[half:, :CUT] - p[:half, CUT:]

    ar, ai = columns(y[:, :CUT])
    br, bi = columns(y[:, CUT:])
    cr = ar * br + ai * bi
    ci = ai * br - ar * bi
    size = jnp.sqrt(cr * cr + ci * ci)
    weighted = (size[:, :128] + size[:, 128:]) * weight[...]
    floor = jnp.sum(weighted) * (1.0 / (ROWS * CUT)) + 1e-06
    scale = 1.0 / (size + floor)
    vr, vi = columns(jnp.concatenate([cr * scale, -ci * scale], axis=0))
    out[...] = left_dot(back3, jnp.concatenate([vr, vi], axis=0))


CHAINS = 4
BAND = ROWS // CHAINS
RING = 8
BLOCK = ROWS // RING
WIDTHS = (1024, 512, 256, 128)
REACH = 3


def first_kernel(
    offsets, raw, *refs,
):
    tables_hbm, refs = refs[:7], refs[7:]
    tables, refs = refs[-9:-2], (*refs[:-9], *refs[-2:])
    (
        out, tile, strip, spec, east,
        sums, west, mine, logs, acc, first, recv1, recv2, recv3, recv4, near, far, hop, spec_y, spec_z, both, load, send, recv,
    ) = refs
    rows3, cols3, twist, rows3_e, back3_e, weight_e, cols3_e = tables
    gz, ta = lax.axis_index("gz"), lax.axis_index("ta")
    y, z = gz // 2, (ta // 8) * 2 + gz % 2
    x, core = (ta // 2) % 4, ta % 2
    other = 1 - core

    loads = []
    for q in range(CHAINS):
        band = pl.ds(q * BAND, BAND)
        c = pltpu.make_async_copy(raw.at[:, band], tile.at[:, band], load.at[q])
        c.start()
        loads.append(c)

    table_loads = []
    for i, (src, dst) in enumerate(zip(tables_hbm, tables)):
        c = pltpu.make_async_copy(src, dst, load.at[CHAINS + i])
        c.start()
        table_loads.append(c)

    def device(x, y, z, core):
        z = (z + RING) % RING
        return (y * 2 + z % 2, (z // 2) * 8 + x * 2 + core)

    def beside(p):
        return p + 1 - 2 * (p % 2)

    def across(p):
        return 3 - p

    def gray(p):
        return (p + p // 2) % 2

    def upper(p):
        return p // 2

    def along(axis, move):
        on_x = (1 - core) if axis == 0 else core
        return device(x + on_x * (move(x) - x), y + (1 - on_x) * (move(y) - y), z, core)

    place = (x + core * (y - x), y + core * (x - y))
    partner_core = device(x, y, z, other)
    partner = {(axis, move): along(axis, move) for axis in (0, 1) for move in (beside, across)}
    down = [device(x, y, z - d, core) for d in range(1, REACH + 1)]
    up = [device(x, y, z + d, core) for d in range(1, REACH + 1)]
    count_ta = lax.axis_size("ta")
    before, after = (gz, (ta + count_ta - 1) % count_ta), (gz, (ta + 1) % count_ta)

    south = (gz, (ta + GRID_COLS) % count_ta)
    north = (gz, (ta + count_ta - GRID_COLS) % count_ta)
    has_south, has_north = ta < count_ta - GRID_COLS, ta >= GRID_COLS
    own_tile = gz * count_ta + ta

    barrier = pltpu.get_barrier_semaphore()
    everyone = [partner_core, *partner.values(), *down, *up, before, after, south, north]
    for d in everyone:
        pl.semaphore_signal(barrier, inc=1, device_id=d, device_id_type=MESH)

    count = [0]
    started = []

    def copy(src, dst, to):
        i = count[0]
        count[0] += 1
        c = pltpu.make_async_remote_copy(
            src_ref=src, dst_ref=dst, send_sem=send.at[i], recv_sem=recv.at[i], device_id=to, device_id_type=MESH
        )
        c.start()
        started.append(c)
        return c

    def band(q):
        return pl.ds(q * BAND, BAND)

    for q in range(CHAINS):
        loads[q].wait()

        def add_planes(i, q=q):
            r = at(q * BAND + i * 8, 8, 8)
            sums[r, :] = tile[0, r, :] + tile[1, r, :]

        loop(BAND // 8, add_planes)

    def cut(i):
        cols = at(i * 128, 128, 128)
        mine[:, cols] = moved(sums[:, cols], offsets[own_tile, 1], 0)[ROWS - CUT :]

    loop(WIDTH // 128, cut)
    pl.semaphore_wait(barrier, len(everyone))
    south_copy = pltpu.make_async_remote_copy(
        src_ref=mine, dst_ref=strip, send_sem=send.at[COPIES], recv_sem=recv.at[COPIES], device_id=south, device_id_type=MESH
    )

    @pl.when(has_south)
    def _():
        south_copy.start()

    @pl.when(jnp.logical_not(has_north))
    def _():
        strip[...] = jnp.zeros_like(strip)

    beside_copy = copy(sums.at[:, pl.ds(0, CUT)], west, before)

    flight = []
    for q in range(CHAINS):

        def take(i, q=q):
            r = at(q * BAND + i * 8, 8, 8)
            for c in range(0, WIDTH, 512):
                cols = slice(c, c + 512)
                one, two = jnp.log(tile[0, r, cols]), jnp.log(tile[1, r, cols])
                logs[0, r, cols] = one + two
                logs[1, r, cols] = jnp.minimum(one, two)

        loop(BAND // 8, take)
        flight.append(copy(logs.at[other, band(q)], first.at[band(q)], partner_core))

    orders = [
        [(0, beside, gray), (0, across, upper), (1, beside, gray), (1, across, upper)],
        [(0, across, upper), (0, beside, gray), (1, across, upper), (1, beside, gray)],
    ]
    moves = [orders[q % 2] for q in range(CHAINS)]
    into = [recv1, recv2, recv3, recv4]
    bases = [[0] for q in range(CHAINS)]
    steps = len(WIDTHS)
    for step in range(steps + 1):
        for q in range(CHAINS):
            flight[q].wait_recv()
            if step == 0:

                def add_first(i, q=q):
                    r = at(q * BAND + i * 8, 8, 8)
                    acc[r, :] = logs[core, r, :] + first[r, :]

                loop(BAND // 8, add_first)
            else:
                w = WIDTHS[step - 1]

                def add_next(i, q=q, c=at(bases[q][step], w, 128), buf=into[step - 1]):
                    r = at(q * BAND + i * 8, 8, 8)
                    acc[r, c] = acc[r, c] + buf[r, :]

                loop(BAND // 8, add_next)
            if step < steps:
                axis, move, bit = moves[q][step]
                w = WIDTHS[step]
                b = bit(place[axis])
                base = bases[q][step]
                flight[q] = copy(
                    acc.at[band(q), at(base + (1 - b) * w, w, 128)], into[step].at[band(q)], partner[(axis, move)]
                )
                bases[q].append(base + b * w)

    def block(shift):
        j = (z + shift + RING) % RING
        col = bases[0][steps] + ((j // 2) % 2) * (bases[1][steps] - bases[0][steps])
        return at(j * BLOCK, BLOCK, 8), at(col, 128, 128)

    fars, nears = [], []
    for d in range(1, REACH + 1):
        r, c = block(4 - d)
        fars.append(copy(acc.at[r, c], far.at[d - 1], down[d - 1]))
    for d in range(1, REACH + 1):
        r, c = block(-d)
        nears.append(copy(acc.at[r, c], near.at[d - 1], down[d - 1]))
    for f in fars:
        f.wait_recv()
    r, c = block(4)
    acc[r, c] = (acc[r, c] + far[0]) + (far[1] + far[2])
    f = copy(acc.at[r, c], hop.at[0], down[2])
    f.wait_recv()
    f = copy(hop.at[0], hop.at[1], down[0])
    for n in nears:
        n.wait_recv()
    r, c = block(0)
    total = (acc[r, c] + near[0]) + (near[1] + near[2])
    f.wait_recv()
    total = total + hop[1]
    is_floor = core.astype(F32)
    scale = is_floor * (1.0 / TILES) - (1.0 - is_floor) * (1.0 / (TILES * PLANES))
    out[core, r, c] = (1.0 - 0.5 * is_floor) * jnp.exp(total * scale)

    def give(r, c, to):
        return copy(out.at[core, r, c], out.at[core, r, c], to)

    ones = [give(*block(0), to) for to in down]
    ones[0].wait_recv()
    f = give(*block(1), down[2])
    f.wait_recv()
    fours = [give(*block(4), to) for to in down]
    for f in ones[1:] + fours:
        f.wait_recv()
    for step in range(steps - 1, -1, -1):
        for q in range(CHAINS):
            if step < steps - 1:
                flight[q].wait_recv()
            axis, move, _ = moves[q][step]
            flight[q] = give(band(q), at(bases[q][step + 1], WIDTHS[step], 128), partner[(axis, move)])
    for q in range(CHAINS):
        flight[q].wait_recv()
        flight[q] = give(band(q), slice(None), partner_core)
    for q in range(CHAINS):
        flight[q].wait_recv()
    beside_copy.wait_recv()

    for c in table_loads:
        c.wait()

    def own_of(cols):
        return (0.5 * sums[:CUT, cols] - out[1, :CUT, cols]) * out[0, :CUT, cols]

    south_forward(own_of, rows3, cols3, twist, spec_y, spec_z, spec)
    has_east = (ta < count_ta - 1).astype(F32)

    def strips(i):
        r, last = at(i * 64, 64, 64), slice(WIDTH - 3 * 128, WIDTH)
        eastern = (0.5 * sums[r, last] - out[1, r, last]) * out[0, r, last]
        both[r, :CUT] = moved(eastern, offsets[own_tile, 0], 1)[:, 128:]
        both[r, CUT:] = (0.5 * west[r, :] - out[1, r, :CUT]) * out[0, r, :CUT] * has_east

    loop(ROWS // 64, strips)
    east_into(east, both[...], rows3_e, back3_e, weight_e, cols3_e)

    @pl.when(has_north)
    def _():
        south_copy.wait_recv()

    for c in started:
        c.wait_send()

    @pl.when(has_south)
    def _():
        south_copy.wait_send()


COPIES = CHAINS * 2 * (1 + len(WIDTHS)) + 1 + (2 * REACH + 2) + (2 * REACH + 1)


VMEM = pl.BlockSpec(memory_space=pltpu.VMEM)
SMEM = pl.BlockSpec(memory_space=pltpu.SMEM)
ANY = pl.BlockSpec(memory_space=pl.ANY)
HBM = pl.BlockSpec(memory_space=pltpu.HBM)
SPEC = (16 * HALF, 256)


def shape(*dims):
    return jax.ShapeDtypeStruct(dims, F32)


def body(raw_planes, offsets):
    rows3, back3, weight, cols3, twist = south_tables()
    rows3_e, back3_e, weight_e, cols3_e = east_tables()
    tables = (rows3, cols3, twist, rows3_e, back3_e, weight_e, cols3_e)
    fields, tile, strip, spec, east = pl.pallas_call(
        first_kernel,
        out_shape=(shape(2, ROWS, WIDTH), shape(PLANES, ROWS, WIDTH), shape(CUT, WIDTH), shape(*SPEC), shape(ROWS, CUT)),
        in_specs=[SMEM] + [HBM] * (1 + len(tables)),
        out_specs=(VMEM,) * 5,
        scratch_shapes=[
            pltpu.VMEM((ROWS, WIDTH), F32),
            pltpu.VMEM((ROWS, CUT), F32),
            pltpu.VMEM((CUT, WIDTH), F32),
            pltpu.VMEM((2, ROWS, WIDTH), F32),
            pltpu.VMEM((ROWS, WIDTH), F32),
            pltpu.VMEM((ROWS, WIDTH), F32),
            *[pltpu.VMEM((ROWS, w), F32) for w in WIDTHS],
            pltpu.VMEM((REACH, BLOCK, 128), F32),
            pltpu.VMEM((REACH, BLOCK, 128), F32),
            pltpu.VMEM((2, BLOCK, 128), F32),
            pltpu.VMEM((2 * HALF, WIDTH), F32),
            pltpu.VMEM(SPEC, F32),
            pltpu.VMEM((ROWS, 2 * CUT), F32),
            pltpu.SemaphoreType.DMA((CHAINS + len(tables),)),
            *[pltpu.VMEM(t.shape, t.dtype) for t in tables],
            pltpu.SemaphoreType.DMA((COPIES + 1,)),
            pltpu.SemaphoreType.DMA((COPIES + 1,)),
        ],
        compiler_params=pltpu.CompilerParams(collective_id=0, has_side_effects=True, vmem_limit_bytes=33 << 20),
        name="first",
    )(offsets, raw_planes[0], *tables)
    corrected, east_corr, south_corr = pl.pallas_call(
        south_kernel,
        out_shape=(shape(PLANES, ROWS, WIDTH), shape(ROWS, CUT), shape(CUT, WIDTH)),
        in_specs=[SMEM] + [VMEM] * 10,
        out_specs=(ANY, ANY, VMEM),
        scratch_shapes=[
            pltpu.VMEM((2 * HALF, WIDTH), F32),
            pltpu.VMEM(SPEC, F32),
            pltpu.VMEM(SPEC, F32),
            pltpu.VMEM((16 * HALF, 128), F32),
            pltpu.VMEM((PLANES, ROWS, WIDTH), F32),
            pltpu.VMEM((CUT, WIDTH), F32),
            pltpu.VMEM((CUT, WIDTH), F32),
            pltpu.SemaphoreType.DMA((2,)),
        ],
        compiler_params=pltpu.CompilerParams(vmem_limit_bytes=24 << 20),
        name="second",
    )(offsets, spec, tile, fields, strip, east, rows3, back3, weight, cols3, twist)
    return (corrected[None], east_corr[None], south_corr[None])


def solution(mesh):
    in_specs = (P(("gz", "ta"), None, None, None), P())
    out_specs = (
        P(("gz", "ta"), None, None, None),
        P(("gz", "ta"), None, None),
        P(("gz", "ta"), None, None),
    )
    return jax.shard_map(body, mesh=mesh, in_specs=in_specs, out_specs=out_specs, check_vma=False)
```

time: 213 us -> 129 us (0.61); the launches traced: 210 us -> 128 us
  Pallas kernels: 163 us -> 120 us
  other arithmetic: 16.9 us -> 0 us
  starting transfers between devices: 9.58 us -> 0 us
  local copies, waits for them, and re-layouts: 15.9 us -> 7.58 us
  between operations: 4.83 us -> 0.68 us
    pallas_call x5 -> x2, Pallas kernels: 163 us -> 120 us  [the longest x1 103 us: body(): pl.pallas_call(first_kernel, out_shape=(shape(2, ROWS, WIDTH), shape(PLAN...]
    ppermute x2 -> x0, starting transfers between devices: 9.58 us -> none  [shifted(): lax.ppermute(value, 'ta', [(source, source + steps) for source in range(f...]
    slice x3 -> x0, local copies, waits for them, and re-layouts: 7.88 us -> none  [the longest x1 4.67 us: body(): inv, dark = (fields[0], fields[1])]
    reduce_sum x4 -> x0, other arithmetic: 7.67 us -> none  [the longest x1 3.18 us: body(): jnp.mean(lax.dynamic_slice_in_dim(tile, ROWS - CUT - own_south, CUT, 1), 0)]
    mul x1 -> x0, other arithmetic: 6.11 us -> none  [body(): corrected = (tile - dark) * inv]
    dynamic_slice x2 -> x0, local copies, waits for them, and re-layouts: 2.89 us -> none  [the longest x1 1.46 us: body(): north_south = offsets[jnp.maximum(own_tile - GRID_COLS, 0), 1]]
    div x4 -> x0, other arithmetic: 2.54 us -> none  [the longest x1 1.54 us: body(): jnp.mean(lax.dynamic_slice_in_dim(tile, ROWS - CUT - own_south, CUT, 1), 0)]
    unnamed x38 -> x19, local copies, waits for them, and re-layouts: 5.13 us -> 7.58 us
  transfers between devices with their start and end apart: 2 -> 0, of which waited for: 0 -> 0; matrix products, arithmetic and copies ran while one was open for 12% -> 0% of each run, Pallas kernels for 71% -> 0%
where the time goes in v2:
time: 129 us; the launch traced here: 128 us
  Pallas kernels  120 us (93%)
  local copies, waits for them, and re-layouts  7.58 us (6%)
    pallas_call x1, Pallas kernels, body(): pl.pallas_call(first_kernel, out_shape=(shape(2, ROWS, WIDTH), shape(PLAN...  103 us
    pallas_call x1, Pallas kernels, body(): pl.pallas_call(south_kernel, out_shape=(shape(PLANES, ROWS, WIDTH), shape...  17.4 us
    unnamed x19, local copies, waits for them, and re-layouts  7.58 us

profile of v2, /device:TPU:1, one launch (start us, length us, event | category | flops | bytes accessed | tf_op | source)
XLA Modules:
  0.0 128.4 jit_solution(16317619622174576527)
XLA Ops:
  0.6 0.0 copy-start.7
  0.6 0.8 copy.15.offsets
  1.5 0.0 copy-start
  1.5 1.0 copy-done
  2.5 0.0 copy-start.1
  2.5 1.0 copy-done.1
  3.5 0.0 copy-start.2
  3.5 1.0 copy-done.2
  4.6 0.0 copy-start.3
  4.6 1.0 copy-done.3
  5.6 0.0 copy-start.4
  5.6 1.0 copy-done.4
  6.6 0.0 copy-start.6
  6.6 0.9 copy-done.6
  7.5 0.0 copy-start.8
  7.5 0.7 copy-done.8
  8.2 0.0 copy-start.5
  8.2 102.8 %first.1 = (f32[2,320,2048]{2,1,0:T(8,128)S(1)}, f32[2,320,2048]{2,1,0:T(8,128)S(1)}, f32[256,2048]{1,0:T(8,128)S(1)}, f32[2304,256]{1,0:T(8,128)S(1)}, f32[320,256]{1,0:T(8,128)S(1)}) custom-call(s32[256,2]{1,0:T(8,128)S(1)} %copy.15.offsets, f32[2,320,2048]{2,1,0:T(8,128)} %bitcast.4, bf16[288,768]{1,0:T(8,128)(2,1)S(1)} %copy-done, ...), custom_call_target="tpu_custom_call" | custom-call | tf_op jit(solution)/shard_map/first/pallas_call | solution.py:561
  111.0 0.0 copy-done.7
  111.0 0.0 copy-done.5
  111.0 17.4 %second.1 = (f32[2,320,2048]{2,1,0:T(8,128)}, f32[320,256]{1,0:T(8,128)}, f32[256,2048]{1,0:T(8,128)}) custom-call(s32[256,2]{1,0:T(8,128)S(1)} %copy.15.offsets, f32[2304,256]{1,0:T(8,128)S(1)} %get-tuple-element.11.own, f32[2,320,2048]{2,1,0:T(8,128)S(1)} %get-tuple-element.12.tile, f32[2,320,2048]{2,1,0:T(8,128)S(1)} %get-tuple-element.13.fields, ...), custom_call_target="tpu_custom_call" | custom-call | tf_op jit(solution)/shard_map/second/pallas_call | solution.py:588
Async XLA Ops:
  0.6 110.4 %copy-start.7 = (f32[144,128]{1,0:T(8,128)S(1)}, f32[144,128]{1,0:T(8,128)}, u32[]{:S(2)}) copy-start(f32[144,128]{1,0:T(8,128)} %constant.26.clone.weight) | copy-start | bytes 221188
  1.5 1.0 copy-start
  2.5 1.0 copy-start.1
  3.5 1.0 copy-start.2
  4.6 1.0 copy-start.3
  5.6 1.0 copy-start.4
  6.6 0.9 copy-start.6
  7.5 0.7 copy-start.8
  8.2 102.8 %copy-start.5 = (bf16[256,864]{1,0:T(8,128)(2,1)S(1)}, bf16[256,864]{1,0:T(8,128)(2,1)}, u32[]{:S(2)}) copy-start(bf16[256,864]{1,0:T(8,128)(2,1)} %constant.25.clone.back3) | copy-start | bytes 1327108

commit v3 on v2

--- a/solution.py
+++ b/solution.py
@@ -28,18 +28,12 @@
     return high, low
 
 
-def stacked(table):
-    return np.stack(two_parts(table))
-
-
-def left_table(table):
-    high, low = two_parts(table)
-    return np.concatenate([high, high, low], axis=1)
-
-
-def right_table(table):
-    high, low = two_parts(table)
-    return np.concatenate([high, high, low], axis=0)
+def three_parts(table):
+    parts = []
+    for _ in range(3):
+        parts.append(table.astype(ml_dtypes.bfloat16))
+        table = table - parts[-1].astype(table.dtype)
+    return parts
 
 
 def angles(rows, cols, length):
@@ -47,38 +41,73 @@
     return product * (2.0 * np.pi / length)
 
 
-def row_tables(length, half, cols, left_table):
+def row_tables(length, cols):
     count = length // 2 + 1
     turn = angles(count, length, length)
-    forward = np.zeros((2 * half, length))
-    forward[:count] = np.cos(turn)
-    forward[half : half + count] = -np.sin(turn)
     weight = np.full((count, 1), 2.0)
     weight[0] = weight[-1] = 1.0
     scale = 1.0 / math.sqrt(length * cols)
-    backward = np.zeros((length, 2 * half))
-    backward[:, :count] = (weight * np.cos(turn)).T * scale
-    backward[:, half : half + count] = (weight * np.sin(turn)).T * scale
-    rows = np.zeros((half, 128), np.float32)
-    rows[:count] = weight
-    return left_table(forward), left_table(backward), rows
-
-
-def south_tables():
-    forward, backward, weight = row_tables(CUT, HALF, WIDTH, left_table)
+    forward = np.cos(turn), -np.sin(turn)
+    backward = (weight * np.cos(turn)).T * scale, (weight * np.sin(turn)).T * scale
+    return forward, backward
+
+
+AT_ROWS, AT_BACK, AT_EAST_ROWS, AT_EAST_BACK, AT_COLS, AT_TWIST, BUNDLE = 0, 256, 512, 864, 1184, 1696, 1728
+
+
+def bundle():
+    out = np.zeros((BUNDLE, 768), ml_dtypes.bfloat16)
+
+    def put(row, col, table):
+        out[row : row + table.shape[0], col : col + table.shape[1]] = table
+
+    (cos, sin), (back_cos, back_sin) = row_tables(CUT, WIDTH)
+    high, low = two_parts(np.concatenate([cos, sin[1:-1]]))
+    put(AT_ROWS, 0, np.concatenate([high, high, low], axis=1))
+    high, low = two_parts(np.concatenate([back_cos, back_sin[:, 1:-1]], axis=1))
+    put(AT_BACK, 0, np.concatenate([high, high, low], axis=1))
+    (cos, sin), (back_cos, back_sin) = row_tables(ROWS, CUT)
+    whole = np.zeros((2 * EAST_HALF, ROWS))
+    whole[: len(cos)], whole[EAST_HALF : EAST_HALF + len(sin)] = cos, sin
+    for i, part in enumerate(two_parts(whole)):
+        put(AT_EAST_ROWS, 384 * i, part)
+    whole = np.zeros((ROWS, 2 * EAST_HALF))
+    whole[:, : len(cos)], whole[:, EAST_HALF : EAST_HALF + len(sin)] = back_cos, back_sin
+    for i, part in enumerate(two_parts(whole)):
+        put(AT_EAST_BACK, 384 * i, part)
+    turn = angles(CUT, CUT, CUT)
+    for i, part in enumerate(two_parts(np.concatenate([np.cos(turn), np.sin(turn)], axis=1))):
+        put(AT_COLS + CUT * i, 0, part)
     turn = angles(128, 128, 128)
     cos, sin = np.cos(turn), np.sin(turn)
-    block = np.block([[cos, -sin], [sin, cos]])
+    for i, part in enumerate(two_parts(np.block([[cos, -sin], [sin, cos]]))):
+        put(AT_COLS + CUT * i, 512, part)
     turn = angles(16, 128, WIDTH)
-    twist = np.concatenate([np.cos(turn), -np.sin(turn)]).astype(np.float32)
-    return forward, backward, weight, right_table(block), twist
-
-
-def east_tables():
-    forward, backward, weight = row_tables(ROWS, EAST_HALF, CUT, stacked)
-    turn = angles(CUT, CUT, CUT)
-    both = np.concatenate([np.cos(turn), np.sin(turn)], axis=1)
-    return forward, backward, weight, stacked(both)
+    for i, part in enumerate(three_parts(np.concatenate([np.cos(turn), -np.sin(turn)]).astype(np.float32))):
+        put(AT_TWIST, 128 * i, part)
+    return out
+
+
+def table_rows3(t):
+    return t[AT_ROWS : AT_ROWS + 256, :]
+
+
+def table_back3(t):
+    return t[AT_BACK : AT_BACK + 256, :]
+
+
+def table_cols3(t):
+    high = t[AT_COLS : AT_COLS + 256, 512:]
+    return jnp.concatenate([high, high, t[AT_COLS + 256 : AT_COLS + 512, 512:]], axis=0)
+
+
+def table_twist(t):
+    parts = [t[AT_TWIST : AT_TWIST + 32, 128 * i : 128 * i + 128].astype(F32) for i in range(3)]
+    return (parts[0] + parts[1]) + parts[2]
+
+
+def pair_of(t, row, rows, cols):
+    return t[row : row + rows, :cols], t[row : row + rows, 384 : 384 + cols]
 
 
 def dot(a, b):
@@ -148,15 +177,19 @@
     return x
 
 
-def aligned(start):
-    base = jnp.minimum(start // 8 * 8, ROWS - CUT - 8)
-    return base, (16 - (start - base)) % 16
-
-
-def south_forward(strip_of, rows3, cols3, twist, y, z, spec):
+def south_forward(strip_of, t, twist, y, z, spec):
+    twist[...] = table_twist(t)
+    for r in (128, HALF + 128):
+        y[r : r + 16, :] = jnp.zeros((16, WIDTH), F32)
+    top = lax.broadcasted_iota(jnp.int32, (8, 256), 0) == 0
+
     def rows_step(i):
         cols = at(i * 256, 256, 256)
-        y[:, cols] = dot(rows3[...], three(strip_of(cols), 0))
+        d = dot(table_rows3(t), three(strip_of(cols), 0))
+        y[:128, cols] = d[:128]
+        y[128:136, cols] = jnp.where(top, d[128:136], 0.0)
+        y[HALF : HALF + 8, cols] = jnp.where(top, 0.0, d[128:136])
+        y[HALF + 8 : HALF + 128, cols] = d[136:]
 
     loop(8, rows_step)
 
@@ -175,48 +208,25 @@
 
     def cols_step(i):
         to = at(i * 576, 576, 8)
-        spec[to, :] = dot(three(z[to, :], 1), cols3[...])
+        spec[to, :] = dot(three(z[to, :], 1), table_cols3(t))
 
     loop(4, cols_step)
 
 
-def south_kernel(
-    offsets, own, tile, fields, strip, east, rows3, back3, weight, cols3, twist,
-    corrected, east_out, out, y, z, spec, mag, ready, inv, dark, sems,
-):
-    slot = lax.axis_index("ta")
-    north = jnp.maximum(lax.axis_index("gz") * lax.axis_size("ta") + slot - GRID_COLS, 0)
-    start = ROWS - CUT - offsets[north, 1]
-    has_north = (slot >= GRID_COLS).astype(F32)
-
-    def correct(i):
-        r = at(i * 8, 8, 8)
-        for c in range(0, WIDTH, 512):
-            cols = slice(c, c + 512)
-            g, d = fields[0, r, cols], fields[1, r, cols]
-            for p in range(PLANES):
-                ready[p, r, cols] = (tile[p, r, cols] - d) * g
-
-    loop(ROWS // 8, correct)
+def half_weight(first, rows, last):
+    h = first + lax.broadcasted_iota(jnp.int32, (rows, 128), 0)
+    return jnp.where(h < last, jnp.where(h == 0, 1.0, 2.0), jnp.where(h == last, 1.0, 0.0))
+
+
+def south_kernel(own, ready, east, strip, inv, dark, t, corrected, east_out, out, y, z, spec, mag, twist, sems):
     writes = [pltpu.make_async_copy(ready, corrected, sems.at[0]), pltpu.make_async_copy(east, east_out, sems.at[1])]
     for w in writes:
         w.start()
 
-    base, turn = aligned(start)
-
-    def cut(i):
-        for c in range(0, WIDTH, 512):
-            cols = slice(c, c + 512)
-            window = at(base + i * 8, 16, 8)
-            inv[at(i * 8, 8, 8), cols] = pltpu.roll(fields[0, window, cols], turn, 0)[:8] * has_north
-            dark[at(i * 8, 8, 8), cols] = pltpu.roll(fields[1, window, cols], turn, 0)[:8]
-
-    loop(CUT // 8, cut)
-
     def strip_of(cols):
         return (0.5 * strip[:, cols] - dark[:, cols]) * inv[:, cols]
 
-    south_forward(strip_of, rows3, cols3, twist, y, z, spec)
+    south_forward(strip_of, t, twist, y, z, spec)
 
     def cross_step(i, total):
         part = jnp.zeros((8, 128), F32)
@@ -231,7 +241,7 @@
             z[here, 128:] = -ci
             mag[here, :] = size
             part = part + size
-        return total + part * weight[at(i * 8, 8, 8), :]
+        return total + part * half_weight(i * 8, 8, CUT // 2)
 
     total = lax.fori_loop(0, HALF // 8, cross_step, jnp.zeros((8, 128), F32))
     floor = jnp.sum(total) * (1.0 / (CUT * WIDTH)) + 1e-06
@@ -240,7 +250,7 @@
         here = at(i * 288, 288, 8)
         scale = 1.0 / (mag[here, :] + floor)
         x = jnp.concatenate([z[here, :128] * scale, z[here, 128:] * scale], axis=1)
-        spec[here, :] = dot(three(x, 1), cols3[...])
+        spec[here, :] = dot(three(x, 1), table_cols3(t))
 
     loop(8, cols_step)
 
@@ -260,21 +270,27 @@
 
     loop(HALF // 8, turn_step)
 
+    top = lax.broadcasted_iota(jnp.int32, (8, 256), 0) == 0
+
     def rows_step(i):
         cols = at(i * 256, 256, 256)
-        out[:, cols] = dot(back3[...], three(y[:, cols], 0))
+        nyquist = y[128:136, cols]
+        first = jnp.where(top, nyquist, y[HALF : HALF + 8, cols])
+        x = jnp.concatenate([y[:128, cols], first, y[HALF + 8 : HALF + 128, cols]], axis=0)
+        out[:, cols] = dot(table_back3(t), three(x, 0))
 
     loop(8, rows_step)
     for w in writes:
         w.wait()
 
 
-def east_into(out, x, rows3, back3, weight, cols3):
+def east_into(out, x, t):
     half = EAST_HALF
-    y = left_dot(rows3, x)
+    y = left_dot(pair_of(t, AT_EAST_ROWS, 2 * half, ROWS), x)
+    cols = t[AT_COLS : AT_COLS + CUT, :512], t[AT_COLS + CUT : AT_COLS + 2 * CUT, :512]
 
     def columns(v):
-        p = right_dot(v, cols3)
+        p = right_dot(v, cols)
         return p[:half, :CUT] + p[half:, CUT:], p[half:, :CUT] - p[:half, CUT:]
 
     ar, ai = columns(y[:, :CUT])
@@ -282,11 +298,11 @@
     cr = ar * br + ai * bi
     ci = ai * br - ar * bi
     size = jnp.sqrt(cr * cr + ci * ci)
-    weighted = (size[:, :128] + size[:, 128:]) * weight[...]
+    weighted = (size[:, :128] + size[:, 128:]) * half_weight(0, half, ROWS // 2)
     floor = jnp.sum(weighted) * (1.0 / (ROWS * CUT)) + 1e-06
     scale = 1.0 / (size + floor)
     vr, vi = columns(jnp.concatenate([cr * scale, -ci * scale], axis=0))
-    out[...] = left_dot(back3, jnp.concatenate([vr, vi], axis=0))
+    out[...] = left_dot(pair_of(t, AT_EAST_BACK, ROWS, 2 * half), jnp.concatenate([vr, vi], axis=0))
 
 
 CHAINS = 4
@@ -298,15 +314,11 @@
 
 
 def first_kernel(
-    offsets, raw, *refs,
+    offsets, raw, bundled,
+    tile, strip, spec, east, inv_south, dark_south, t,
+    out, sums, west, mine, logs, acc, first, recv1, recv2, recv3, recv4, near, far, hop, spec_y, spec_z, both, twist,
+    load, send, recv,
 ):
-    tables_hbm, refs = refs[:7], refs[7:]
-    tables, refs = refs[-9:-2], (*refs[:-9], *refs[-2:])
-    (
-        out, tile, strip, spec, east,
-        sums, west, mine, logs, acc, first, recv1, recv2, recv3, recv4, near, far, hop, spec_y, spec_z, both, load, send, recv,
-    ) = refs
-    rows3, cols3, twist, rows3_e, back3_e, weight_e, cols3_e = tables
     gz, ta = lax.axis_index("gz"), lax.axis_index("ta")
     y, z = gz // 2, (ta // 8) * 2 + gz % 2
     x, core = (ta // 2) % 4, ta % 2
@@ -319,11 +331,8 @@
         c.start()
         loads.append(c)
 
-    table_loads = []
-    for i, (src, dst) in enumerate(zip(tables_hbm, tables)):
-        c = pltpu.make_async_copy(src, dst, load.at[CHAINS + i])
-        c.start()
-        table_loads.append(c)
+    table_load = pltpu.make_async_copy(bundled, t, load.at[CHAINS])
+    table_load.start()
 
     def device(x, y, z, core):
         z = (z + RING) % RING
@@ -408,6 +417,13 @@
 
     beside_copy = copy(sums.at[:, pl.ds(0, CUT)], west, before)
 
+    orders = [
+        [(0, beside, gray), (0, across, upper), (1, beside, gray), (1, across, upper)],
+        [(0, across, upper), (0, beside, gray), (1, across, upper), (1, beside, gray)],
+    ]
+    moves = [orders[q % 2] for q in range(CHAINS)]
+    into = [recv1, recv2, recv3, recv4]
+    bases = [[0] for q in range(CHAINS)]
     flight = []
     for q in range(CHAINS):
 
@@ -420,34 +436,38 @@
                 logs[1, r, cols] = jnp.minimum(one, two)
 
         loop(BAND // 8, take)
-        flight.append(copy(logs.at[other, band(q)], first.at[band(q)], partner_core))
-
-    orders = [
-        [(0, beside, gray), (0, across, upper), (1, beside, gray), (1, across, upper)],
-        [(0, across, upper), (0, beside, gray), (1, across, upper), (1, beside, gray)],
-    ]
-    moves = [orders[q % 2] for q in range(CHAINS)]
-    into = [recv1, recv2, recv3, recv4]
-    bases = [[0] for q in range(CHAINS)]
+        bit = moves[q][0][2](place[1])
+        halves = [at((1 - bit) * 1024, 1024, 128), at(bit * 1024, 1024, 128)]
+        flight.append([copy(logs.at[other, band(q), c], first.at[band(q), c], partner_core) for c in halves])
+
     steps = len(WIDTHS)
-    for step in range(steps + 1):
+    for q in range(CHAINS):
+
+        def add_first(i, q=q, c=0):
+            r = at(q * BAND + i * 8, 8, 8)
+            acc[r, c] = logs[core, r, c] + first[r, c]
+
+        halves = flight[q]
+        axis, move, bit = moves[q][0]
+        b = bit(place[axis])
+        c = at((1 - b) * 1024, 1024, 128)
+        halves[0].wait_recv()
+        loop(BAND // 8, lambda i, q=q, c=c: add_first(i, q, c))
+        flight[q] = copy(acc.at[band(q), c], into[0].at[band(q)], partner[(axis, move)])
+        c = at(b * 1024, 1024, 128)
+        halves[1].wait_recv()
+        loop(BAND // 8, lambda i, q=q, c=c: add_first(i, q, c))
+        bases[q].append(b * 1024)
+    for step in range(1, steps + 1):
         for q in range(CHAINS):
             flight[q].wait_recv()
-            if step == 0:
-
-                def add_first(i, q=q):
-                    r = at(q * BAND + i * 8, 8, 8)
-                    acc[r, :] = logs[core, r, :] + first[r, :]
-
-                loop(BAND // 8, add_first)
-            else:
-                w = WIDTHS[step - 1]
-
-                def add_next(i, q=q, c=at(bases[q][step], w, 128), buf=into[step - 1]):
-                    r = at(q * BAND + i * 8, 8, 8)
-                    acc[r, c] = acc[r, c] + buf[r, :]
-
-                loop(BAND // 8, add_next)
+            w = WIDTHS[step - 1]
+
+            def add_next(i, q=q, c=at(bases[q][step], w, 128), buf=into[step - 1]):
+                r = at(q * BAND + i * 8, 8, 8)
+                acc[r, c] = acc[r, c] + buf[r, :]
+
+            loop(BAND // 8, add_next)
             if step < steps:
                 axis, move, bit = moves[q][step]
                 w = WIDTHS[step]
@@ -497,26 +517,35 @@
     fours = [give(*block(4), to) for to in down]
     for f in ones[1:] + fours:
         f.wait_recv()
+    passed = []
+
+    def pass_on(q, base, w):
+        passed.append(give(band(q), at(base, w, 128), partner_core))
+
     for step in range(steps - 1, -1, -1):
         for q in range(CHAINS):
+            w = WIDTHS[step]
             if step < steps - 1:
                 flight[q].wait_recv()
             axis, move, _ = moves[q][step]
-            flight[q] = give(band(q), at(bases[q][step + 1], WIDTHS[step], 128), partner[(axis, move)])
+            flight[q] = give(band(q), at(bases[q][step + 1], w, 128), partner[(axis, move)])
+            if step == steps - 1:
+                pass_on(q, bases[q][steps], w)
+            else:
+                pass_on(q, 2 * bases[q][step + 1] + WIDTHS[step + 1] - bases[q][step + 2], WIDTHS[step + 1])
     for q in range(CHAINS):
         flight[q].wait_recv()
-        flight[q] = give(band(q), slice(None), partner_core)
-    for q in range(CHAINS):
-        flight[q].wait_recv()
+        pass_on(q, WIDTHS[0] - bases[q][1], WIDTHS[0])
+    for c in passed:
+        c.wait_recv()
     beside_copy.wait_recv()
 
-    for c in table_loads:
-        c.wait()
+    table_load.wait()
 
     def own_of(cols):
         return (0.5 * sums[:CUT, cols] - out[1, :CUT, cols]) * out[0, :CUT, cols]
 
-    south_forward(own_of, rows3, cols3, twist, spec_y, spec_z, spec)
+    south_forward(own_of, t, twist, spec_y, spec_z, spec)
     has_east = (ta < count_ta - 1).astype(F32)
 
     def strips(i):
@@ -526,7 +555,27 @@
         both[r, CUT:] = (0.5 * west[r, :] - out[1, r, :CUT]) * out[0, r, :CUT] * has_east
 
     loop(ROWS // 64, strips)
-    east_into(east, both[...], rows3_e, back3_e, weight_e, cols3_e)
+    east_into(east, both[...], t)
+
+    def correct(i):
+        r = at(i * 8, 8, 8)
+        for c in range(0, WIDTH, 512):
+            cols = slice(c, c + 512)
+            g, d = out[0, r, cols], out[1, r, cols]
+            for p in range(PLANES):
+                tile[p, r, cols] = (tile[p, r, cols] - d) * g
+
+    loop(ROWS // 8, correct)
+    north_tile = jnp.maximum(own_tile - GRID_COLS, 0)
+    north_is = has_north.astype(F32)
+
+    def cut_fields(i):
+        cols = at(i * 128, 128, 128)
+        steps = offsets[north_tile, 1]
+        inv_south[:, cols] = moved(out[0, :, cols], steps, 0)[ROWS - CUT :] * north_is
+        dark_south[:, cols] = moved(out[1, :, cols], steps, 0)[ROWS - CUT :]
+
+    loop(WIDTH // 128, cut_fields)
 
     @pl.when(has_north)
     def _():
@@ -540,7 +589,7 @@
         south_copy.wait_send()
 
 
-COPIES = CHAINS * 2 * (1 + len(WIDTHS)) + 1 + (2 * REACH + 2) + (2 * REACH + 1)
+COPIES = CHAINS * (2 * len(WIDTHS) + 2 + len(WIDTHS) + 1) + 1 + (2 * REACH + 2) + (2 * REACH + 1)
 
 
 VMEM = pl.BlockSpec(memory_space=pltpu.VMEM)
@@ -548,6 +597,7 @@
 ANY = pl.BlockSpec(memory_space=pl.ANY)
 HBM = pl.BlockSpec(memory_space=pltpu.HBM)
 SPEC = (16 * HALF, 256)
+FIRST_LIMIT = 34
 
 
 def shape(*dims):
@@ -555,15 +605,16 @@
 
 
 def body(raw_planes, offsets):
-    rows3, back3, weight, cols3, twist = south_tables()
-    rows3_e, back3_e, weight_e, cols3_e = east_tables()
-    tables = (rows3, cols3, twist, rows3_e, back3_e, weight_e, cols3_e)
-    fields, tile, strip, spec, east = pl.pallas_call(
+    table = jax.ShapeDtypeStruct((BUNDLE, 768), BF16)
+    ready, strip, spec, east, inv, dark, tables = pl.pallas_call(
         first_kernel,
-        out_shape=(shape(2, ROWS, WIDTH), shape(PLANES, ROWS, WIDTH), shape(CUT, WIDTH), shape(*SPEC), shape(ROWS, CUT)),
-        in_specs=[SMEM] + [HBM] * (1 + len(tables)),
-        out_specs=(VMEM,) * 5,
+        out_shape=(
+            shape(PLANES, ROWS, WIDTH), shape(CUT, WIDTH), shape(*SPEC), shape(ROWS, CUT), shape(CUT, WIDTH), shape(CUT, WIDTH), table,
+        ),
+        in_specs=[SMEM, ANY, ANY],
+        out_specs=(VMEM,) * 7,
         scratch_shapes=[
+            pltpu.VMEM((2, ROWS, WIDTH), F32),
             pltpu.VMEM((ROWS, WIDTH), F32),
             pltpu.VMEM((ROWS, CUT), F32),
             pltpu.VMEM((CUT, WIDTH), F32),
@@ -577,32 +628,30 @@
             pltpu.VMEM((2 * HALF, WIDTH), F32),
             pltpu.VMEM(SPEC, F32),
             pltpu.VMEM((ROWS, 2 * CUT), F32),
-            pltpu.SemaphoreType.DMA((CHAINS + len(tables),)),
-            *[pltpu.VMEM(t.shape, t.dtype) for t in tables],
+            pltpu.VMEM((32, 128), F32),
+            pltpu.SemaphoreType.DMA((CHAINS + 1,)),
             pltpu.SemaphoreType.DMA((COPIES + 1,)),
             pltpu.SemaphoreType.DMA((COPIES + 1,)),
         ],
-        compiler_params=pltpu.CompilerParams(collective_id=0, has_side_effects=True, vmem_limit_bytes=33 << 20),
+        compiler_params=pltpu.CompilerParams(collective_id=0, has_side_effects=True, vmem_limit_bytes=FIRST_LIMIT << 20),
         name="first",
-    )(offsets, raw_planes[0], *tables)
+    )(offsets, raw_planes[0], bundle())
     corrected, east_corr, south_corr = pl.pallas_call(
         south_kernel,
         out_shape=(shape(PLANES, ROWS, WIDTH), shape(ROWS, CUT), shape(CUT, WIDTH)),
-        in_specs=[SMEM] + [VMEM] * 10,
+        in_specs=[VMEM] * 7,
         out_specs=(ANY, ANY, VMEM),
         scratch_shapes=[
             pltpu.VMEM((2 * HALF, WIDTH), F32),
             pltpu.VMEM(SPEC, F32),
             pltpu.VMEM(SPEC, F32),
             pltpu.VMEM((16 * HALF, 128), F32),
-            pltpu.VMEM((PLANES, ROWS, WIDTH), F32),
-            pltpu.VMEM((CUT, WIDTH), F32),
-            pltpu.VMEM((CUT, WIDTH), F32),
+            pltpu.VMEM((32, 128), F32),
             pltpu.SemaphoreType.DMA((2,)),
         ],
-        compiler_params=pltpu.CompilerParams(vmem_limit_bytes=24 << 20),
+        compiler_params=pltpu.CompilerParams(vmem_limit_bytes=20 << 20),
         name="second",
-    )(offsets, spec, tile, fields, strip, east, rows3, back3, weight, cols3, twist)
+    )(spec, ready, east, strip, inv, dark, tables)
     return (corrected[None], east_corr[None], south_corr[None])
 
 

time: 129 us -> 120 us (0.930)
  local copies, waits for them, and re-layouts: 7.58 us -> 2.56 us
  Pallas kernels: 120 us -> 116 us
    unnamed x19 -> x3, local copies, waits for them, and re-layouts: 7.58 us -> 2.56 us
    pallas_call x1, Pallas kernels: 17.4 us -> 12.6 us  [body(): pl.pallas_call(south_kernel, out_shape=(shape(PLANES, ROWS, WIDTH), shape...]
where the time goes in v3:
time: 120 us
  Pallas kernels  116 us (97%)
  local copies, waits for them, and re-layouts  2.56 us (2%)
    pallas_call x1, Pallas kernels, body(): pl.pallas_call(first_kernel, out_shape=(shape(PLANES, ROWS, WIDTH), shape...  104 us
    pallas_call x1, Pallas kernels, body(): pl.pallas_call(south_kernel, out_shape=(shape(PLANES, ROWS, WIDTH), shape...  12.6 us
    unnamed x3, local copies, waits for them, and re-layouts  2.56 us

profile of v3, /device:TPU:1, one launch (start us, length us, event | category | flops | bytes accessed | tf_op | source)
XLA Modules:
  0.0 119.7 jit_solution(3814383112235690357)
XLA Ops:
  0.6 0.8 copy.6.offsets
  1.4 0.0 copy-start
  1.5 1.7 %copy-done = bf16[1728,768]{1,0:T(8,128)(2,1)S(1)} copy-done((bf16[1728,768]{1,0:T(8,128)(2,1)S(1)}, bf16[1728,768]{1,0:T(8,128)(2,1)}, u32[]{:S(2)}) %copy-start) | copy-done | bytes 2654232
  3.2 103.9 %first.1 = (f32[2,320,2048]{2,1,0:T(8,128)S(1)}, f32[256,2048]{1,0:T(8,128)S(1)}, f32[2304,256]{1,0:T(8,128)S(1)}, f32[320,256]{1,0:T(8,128)S(1)}, f32[256,2048]...) custom-call(s32[256,2]{1,0:T(8,128)S(1)} %copy.6.offsets, f32[2,320,2048]{2,1,0:T(8,128)} %bitcast.4, ...), custom_call_target="tpu_custom_call" | custom-call | tf_op jit(solution)/shard_map/first/pallas_call | solution.py:609
  107.1 12.6 %second.1 = (f32[2,320,2048]{2,1,0:T(8,128)}, f32[320,256]{1,0:T(8,128)}, f32[256,2048]{1,0:T(8,128)}) custom-call(f32[2304,256]{1,0:T(8,128)S(1)} %get-tuple-element.13.own, f32[2,320,2048]{2,1,0:T(8,128)S(1)} %get-tuple-element.14.ready, f32[320,256]{1,0:T(8,128)S(1)} %get-tuple-element.15.east, f32[256,2048]{1,0:T(8,128)S(1)} %get-tuple-element.16.strip, ...), custom_call_target="tpu_custom_call" | custom-call | tf_op jit(solution)/shard_map/second/pallas_call | solution.py:639
Async XLA Ops:
  1.4 1.8 %copy-start = (bf16[1728,768]{1,0:T(8,128)(2,1)S(1)}, bf16[1728,768]{1,0:T(8,128)(2,1)}, u32[]{:S(2)}) copy-start(bf16[1728,768]{1,0:T(8,128)(2,1)} %constant.2.clone.bundled) | copy-start | bytes 7962628

commit v4 on v3

--- a/solution.py
+++ b/solution.py
@@ -19,6 +19,7 @@
 EAST_HALF = 176
 MESH = pl.DeviceIdType.MESH
 F32 = jnp.float32
+U_ROWS, U_COLS, U_TURN = 8, 4, 1
 BF16 = jnp.bfloat16
 
 
@@ -166,8 +167,13 @@
     return pl.ds(pl.multiple_of(start, step), size)
 
 
-def loop(count, f):
-    lax.fori_loop(0, count, lambda i, c: (f(i), c)[1], 0)
+def loop(count, f, at_once=1):
+    def step(i, c):
+        for j in range(at_once):
+            f(i * at_once + j)
+        return c
+
+    lax.fori_loop(0, count // at_once, step, 0)
 
 
 def moved(x, steps, axis):
@@ -191,7 +197,7 @@
         y[HALF : HALF + 8, cols] = jnp.where(top, 0.0, d[128:136])
         y[HALF + 8 : HALF + 128, cols] = d[136:]
 
-    loop(8, rows_step)
+    loop(8, rows_step, U_ROWS)
 
     def turn_step(i):
         top, low = at(i * 8, 8, 8), at(HALF + i * 8, 8, 8)
@@ -204,13 +210,13 @@
             z[to, :128] = re[k] * c - im[k] * s
             z[to, 128:] = re[k] * s + im[k] * c
 
-    loop(HALF // 8, turn_step)
+    loop(HALF // 8, turn_step, U_TURN)
 
     def cols_step(i):
         to = at(i * 576, 576, 8)
         spec[to, :] = dot(three(z[to, :], 1), table_cols3(t))
 
-    loop(4, cols_step)
+    loop(4, cols_step, U_COLS)
 
 
 def half_weight(first, rows, last):
@@ -252,7 +258,7 @@
         x = jnp.concatenate([z[here, :128] * scale, z[here, 128:] * scale], axis=1)
         spec[here, :] = dot(three(x, 1), table_cols3(t))
 
-    loop(8, cols_step)
+    loop(8, cols_step, 2 * U_COLS)
 
     def turn_step(i):
         re, im = [], []
@@ -268,7 +274,7 @@
             y[top, 128 * a : 128 * a + 128] = re[a]
             y[low, 128 * a : 128 * a + 128] = im[a]
 
-    loop(HALF // 8, turn_step)
+    loop(HALF // 8, turn_step, U_TURN)
 
     top = lax.broadcasted_iota(jnp.int32, (8, 256), 0) == 0
 
@@ -279,7 +285,7 @@
         x = jnp.concatenate([y[:128, cols], first, y[HALF + 8 : HALF + 128, cols]], axis=0)
         out[:, cols] = dot(table_back3(t), three(x, 0))
 
-    loop(8, rows_step)
+    loop(8, rows_step, U_ROWS)
     for w in writes:
         w.wait()
 

time: 120 us -> 114 us (0.950)
  Pallas kernels: 116 us -> 111 us
    pallas_call x1, Pallas kernels: 12.6 us -> 8.38 us  [body(): pl.pallas_call(south_kernel, out_shape=(shape(PLANES, ROWS, WIDTH), shape...]
    pallas_call x1, Pallas kernels: 104 us -> 102 us  [body(): pl.pallas_call(first_kernel, out_shape=(shape(PLANES, ROWS, WIDTH), shape...]
where the time goes in v4:
time: 114 us
  Pallas kernels  111 us (97%)
  local copies, waits for them, and re-layouts  2.56 us (2%)
    pallas_call x1, Pallas kernels, body(): pl.pallas_call(first_kernel, out_shape=(shape(PLANES, ROWS, WIDTH), shape...  102 us
    pallas_call x1, Pallas kernels, body(): pl.pallas_call(south_kernel, out_shape=(shape(PLANES, ROWS, WIDTH), shape...  8.38 us
    unnamed x3, local copies, waits for them, and re-layouts  2.56 us

profile of v4, /device:TPU:1, one launch (start us, length us, event | category | flops | bytes accessed | tf_op | source)
XLA Modules:
  0.0 113.7 jit_solution(7293043306769129865)
XLA Ops:
  0.6 0.8 copy.6.offsets
  1.4 0.0 copy-start
  1.5 1.7 %copy-done = bf16[1728,768]{1,0:T(8,128)(2,1)S(1)} copy-done((bf16[1728,768]{1,0:T(8,128)(2,1)S(1)}, bf16[1728,768]{1,0:T(8,128)(2,1)}, u32[]{:S(2)}) %copy-start) | copy-done | bytes 2654232
  3.2 102.1 %first.1 = (f32[2,320,2048]{2,1,0:T(8,128)S(1)}, f32[256,2048]{1,0:T(8,128)S(1)}, f32[2304,256]{1,0:T(8,128)S(1)}, f32[320,256]{1,0:T(8,128)S(1)}, f32[256,2048]...) custom-call(s32[256,2]{1,0:T(8,128)S(1)} %copy.6.offsets, f32[2,320,2048]{2,1,0:T(8,128)} %bitcast.4, ...), custom_call_target="tpu_custom_call" | custom-call | tf_op jit(solution)/shard_map/first/pallas_call | solution.py:615
  105.4 8.4 %second.1 = (f32[2,320,2048]{2,1,0:T(8,128)}, f32[320,256]{1,0:T(8,128)}, f32[256,2048]{1,0:T(8,128)}) custom-call(f32[2304,256]{1,0:T(8,128)S(1)} %get-tuple-element.13.own, f32[2,320,2048]{2,1,0:T(8,128)S(1)} %get-tuple-element.14.ready, f32[320,256]{1,0:T(8,128)S(1)} %get-tuple-element.15.east, f32[256,2048]{1,0:T(8,128)S(1)} %get-tuple-element.16.strip, ...), custom_call_target="tpu_custom_call" | custom-call | tf_op jit(solution)/shard_map/second/pallas_call | solution.py:645
Async XLA Ops:
  1.4 1.8 %copy-start = (bf16[1728,768]{1,0:T(8,128)(2,1)S(1)}, bf16[1728,768]{1,0:T(8,128)(2,1)}, u32[]{:S(2)}) copy-start(bf16[1728,768]{1,0:T(8,128)(2,1)} %constant.2.clone.bundled) | copy-start | bytes 7962628

commit v5 on v4

--- a/solution.py
+++ b/solution.py
@@ -183,6 +183,28 @@
     return x
 
 
+def fold(to, whole, offset, factor=None):
+    def scaled(x):
+        return x if factor is None else x * factor
+
+    start = ROWS - CUT - offset
+
+    def low(i):
+        r = at(i * 8, 8, 8)
+        rest = jnp.full((8, 512), start - i * 8, jnp.int32)
+        late = lax.broadcasted_iota(jnp.int32, (8, 512), 0) < rest
+        for c in range(0, WIDTH, 512):
+            cols = slice(c, c + 512)
+            to[r, cols] = scaled(jnp.where(late, whole[at(CUT + i * 8, 8, 8), cols], whole[r, cols]))
+
+    def high(i):
+        r = at(ROWS - CUT + i * 8, 8, 8)
+        to[r, :] = scaled(whole[r, :])
+
+    loop((ROWS - CUT) // 8, low)
+    loop((2 * CUT - ROWS) // 8, high)
+
+
 def south_forward(strip_of, t, twist, y, z, spec):
     twist[...] = table_twist(t)
     for r in (128, HALF + 128):
@@ -224,10 +246,15 @@
     return jnp.where(h < last, jnp.where(h == 0, 1.0, 2.0), jnp.where(h == last, 1.0, 0.0))
 
 
-def south_kernel(own, ready, east, strip, inv, dark, t, corrected, east_out, out, y, z, spec, mag, twist, sems):
+def south_kernel(offsets, own, ready, east, strip, inv, dark, t, corrected, east_out, out, y, z, spec, mag, twist, phase, sems):
     writes = [pltpu.make_async_copy(ready, corrected, sems.at[0]), pltpu.make_async_copy(east, east_out, sems.at[1])]
     for w in writes:
         w.start()
+
+    north = jnp.maximum(lax.axis_index("gz") * lax.axis_size("ta") + lax.axis_index("ta") - GRID_COLS, 0)
+    start = ROWS - CUT - offsets[1, north]
+    angle = (lax.broadcasted_iota(jnp.int32, (HALF, 128), 0) * start & (CUT - 1)).astype(F32) * (2.0 * math.pi / CUT)
+    phase[0], phase[1] = jnp.cos(angle), jnp.sin(angle)
 
     def strip_of(cols):
         return (0.5 * strip[:, cols] - dark[:, cols]) * inv[:, cols]
@@ -270,9 +297,10 @@
             im.append(a * s + b * c)
         re, im = butterfly(re, im)
         top, low = at(i * 8, 8, 8), at(HALF + i * 8, 8, 8)
+        c, s = phase[0, top, :], phase[1, top, :]
         for a in range(16):
-            y[top, 128 * a : 128 * a + 128] = re[a]
-            y[low, 128 * a : 128 * a + 128] = im[a]
+            y[top, 128 * a : 128 * a + 128] = re[a] * c - im[a] * s
+            y[low, 128 * a : 128 * a + 128] = re[a] * s + im[a] * c
 
     loop(HALF // 8, turn_step, U_TURN)
 
@@ -403,11 +431,7 @@
 
         loop(BAND // 8, add_planes)
 
-    def cut(i):
-        cols = at(i * 128, 128, 128)
-        mine[:, cols] = moved(sums[:, cols], offsets[own_tile, 1], 0)[ROWS - CUT :]
-
-    loop(WIDTH // 128, cut)
+    fold(mine, sums, offsets[1, own_tile])
     pl.semaphore_wait(barrier, len(everyone))
     south_copy = pltpu.make_async_remote_copy(
         src_ref=mine, dst_ref=strip, send_sem=send.at[COPIES], recv_sem=recv.at[COPIES], device_id=south, device_id_type=MESH
@@ -557,7 +581,7 @@
     def strips(i):
         r, last = at(i * 64, 64, 64), slice(WIDTH - 3 * 128, WIDTH)
         eastern = (0.5 * sums[r, last] - out[1, r, last]) * out[0, r, last]
-        both[r, :CUT] = moved(eastern, offsets[own_tile, 0], 1)[:, 128:]
+        both[r, :CUT] = moved(eastern, offsets[0, own_tile], 1)[:, 128:]
         both[r, CUT:] = (0.5 * west[r, :] - out[1, r, :CUT]) * out[0, r, :CUT] * has_east
 
     loop(ROWS // 64, strips)
@@ -575,13 +599,8 @@
     north_tile = jnp.maximum(own_tile - GRID_COLS, 0)
     north_is = has_north.astype(F32)
 
-    def cut_fields(i):
-        cols = at(i * 128, 128, 128)
-        steps = offsets[north_tile, 1]
-        inv_south[:, cols] = moved(out[0, :, cols], steps, 0)[ROWS - CUT :] * north_is
-        dark_south[:, cols] = moved(out[1, :, cols], steps, 0)[ROWS - CUT :]
-
-    loop(WIDTH // 128, cut_fields)
+    fold(inv_south, out.at[0], offsets[1, north_tile], north_is)
+    fold(dark_south, out.at[1], offsets[1, north_tile])
 
     @pl.when(has_north)
     def _():
@@ -611,6 +630,7 @@
 
 
 def body(raw_planes, offsets):
+    offsets = offsets.T
     table = jax.ShapeDtypeStruct((BUNDLE, 768), BF16)
     ready, strip, spec, east, inv, dark, tables = pl.pallas_call(
         first_kernel,
@@ -645,7 +665,7 @@
     corrected, east_corr, south_corr = pl.pallas_call(
         south_kernel,
         out_shape=(shape(PLANES, ROWS, WIDTH), shape(ROWS, CUT), shape(CUT, WIDTH)),
-        in_specs=[VMEM] * 7,
+        in_specs=[SMEM] + [VMEM] * 7,
         out_specs=(ANY, ANY, VMEM),
         scratch_shapes=[
             pltpu.VMEM((2 * HALF, WIDTH), F32),
@@ -653,11 +673,12 @@
             pltpu.VMEM(SPEC, F32),
             pltpu.VMEM((16 * HALF, 128), F32),
             pltpu.VMEM((32, 128), F32),
+            pltpu.VMEM((2, HALF, 128), F32),
             pltpu.SemaphoreType.DMA((2,)),
         ],
         compiler_params=pltpu.CompilerParams(vmem_limit_bytes=20 << 20),
         name="second",
-    )(spec, ready, east, strip, inv, dark, tables)
+    )(offsets, spec, ready, east, strip, inv, dark, tables)
     return (corrected[None], east_corr[None], south_corr[None])
 
 

time: 114 us -> 112 us (0.982)
  Pallas kernels: 111 us -> 108 us
    pallas_call x1, Pallas kernels: 102 us -> 99 us  [body(): pl.pallas_call(first_kernel, out_shape=(shape(PLANES, ROWS, WIDTH), shape...]
    unnamed x3 -> x4, local copies, waits for them, and re-layouts: 2.56 us -> 2.43 us
where the time goes in v5:
time: 112 us; the launch traced here: 111 us
  Pallas kernels  108 us (96%)
  local copies, waits for them, and re-layouts  2.43 us (2%)
    pallas_call x1, Pallas kernels, body(): pl.pallas_call(first_kernel, out_shape=(shape(PLANES, ROWS, WIDTH), shape...  99 us
    pallas_call x1, Pallas kernels, body(): pl.pallas_call(south_kernel, out_shape=(shape(PLANES, ROWS, WIDTH), shape...  9.4 us
    unnamed x4, local copies, waits for them, and re-layouts  2.43 us

profile of v5, /device:TPU:1, one launch (start us, length us, event | category | flops | bytes accessed | tf_op | source)
XLA Modules:
  0.0 111.4 jit_solution(16549004026256921992)
XLA Ops:
  0.6 0.0 copy-start
  0.6 1.7 %copy-done = bf16[1728,768]{1,0:T(8,128)(2,1)S(1)} copy-done((bf16[1728,768]{1,0:T(8,128)(2,1)S(1)}, bf16[1728,768]{1,0:T(8,128)(2,1)}, u32[]{:S(2)}) %copy-start) | copy-done | bytes 2654232
  2.4 0.0 copy-start.1
  2.4 0.7 copy-done.1
  3.1 99.0 %first.1 = (f32[2,320,2048]{2,1,0:T(8,128)S(1)}, f32[256,2048]{1,0:T(8,128)S(1)}, f32[2304,256]{1,0:T(8,128)S(1)}, f32[320,256]{1,0:T(8,128)S(1)}, f32[256,2048]...) custom-call(s32[2,256]{1,0:T(2,128)S(1)} %bitcast.5, f32[2,320,2048]{2,1,0:T(8,128)} %bitcast.7, ...), custom_call_target="tpu_custom_call" | custom-call | tf_op jit(solution)/shard_map/first/pallas_call | solution.py:635
  102.0 9.4 %second.1 = (f32[2,320,2048]{2,1,0:T(8,128)}, f32[320,256]{1,0:T(8,128)}, f32[256,2048]{1,0:T(8,128)}) custom-call(s32[2,256]{1,0:T(2,128)S(1)} %bitcast.6, f32[2304,256]{1,0:T(8,128)S(1)} %get-tuple-element.13.own, f32[2,320,2048]{2,1,0:T(8,128)S(1)} %get-tuple-element.14.ready, f32[320,256]{1,0:T(8,128)S(1)} %get-tuple-element.15.east, ...), custom_call_target="tpu_custom_call" | custom-call | tf_op jit(solution)/shard_map/second/pallas_call | solution.py:665
Async XLA Ops:
  0.6 1.8 %copy-start = (bf16[1728,768]{1,0:T(8,128)(2,1)S(1)}, bf16[1728,768]{1,0:T(8,128)(2,1)}, u32[]{:S(2)}) copy-start(bf16[1728,768]{1,0:T(8,128)(2,1)} %constant.2.clone.bundled) | copy-start | bytes 7962628
  2.4 0.7 copy-start.1

commit v6 on v5

--- a/solution.py
+++ b/solution.py
@@ -183,10 +183,11 @@
     return x
 
 
-def fold(to, whole, offset, factor=None):
-    def scaled(x):
-        return x if factor is None else x * factor
-
+def scaled(x, factor):
+    return x if factor is None else x * factor
+
+
+def fold_low(to, whole, offset, factor=None):
     start = ROWS - CUT - offset
 
     def low(i):
@@ -195,14 +196,22 @@
         late = lax.broadcasted_iota(jnp.int32, (8, 512), 0) < rest
         for c in range(0, WIDTH, 512):
             cols = slice(c, c + 512)
-            to[r, cols] = scaled(jnp.where(late, whole[at(CUT + i * 8, 8, 8), cols], whole[r, cols]))
-
+            to[r, cols] = scaled(jnp.where(late, whole[at(CUT + i * 8, 8, 8), cols], whole[r, cols]), factor)
+
+    loop((ROWS - CUT) // 8, low)
+
+
+def fold_high(to, whole, first, last, factor=None):
     def high(i):
-        r = at(ROWS - CUT + i * 8, 8, 8)
-        to[r, :] = scaled(whole[r, :])
-
-    loop((ROWS - CUT) // 8, low)
-    loop((2 * CUT - ROWS) // 8, high)
+        r = at(first + i * 8, 8, 8)
+        to[r, :] = scaled(whole[r, :], factor)
+
+    loop((last - first) // 8, high)
+
+
+def fold(to, whole, offset, factor=None):
+    fold_low(to, whole, offset, factor)
+    fold_high(to, whole, ROWS - CUT, CUT, factor)
 
 
 def south_forward(strip_of, t, twist, y, z, spec):
@@ -422,6 +431,14 @@
     def band(q):
         return pl.ds(q * BAND, BAND)
 
+    pieces = [pl.ds(ROWS - CUT, 2 * BAND - (ROWS - CUT)), pl.ds(2 * BAND, CUT - 2 * BAND), pl.ds(0, ROWS - CUT)]
+    south_copies = [
+        pltpu.make_async_remote_copy(
+            src_ref=mine.at[p], dst_ref=strip.at[p], send_sem=send.at[COPIES + i], recv_sem=recv.at[COPIES + i],
+            device_id=south, device_id_type=MESH,
+        )
+        for i, p in enumerate(pieces)
+    ]
     for q in range(CHAINS):
         loads[q].wait()
 
@@ -430,16 +447,21 @@
             sums[r, :] = tile[0, r, :] + tile[1, r, :]
 
         loop(BAND // 8, add_planes)
-
-    fold(mine, sums, offsets[1, own_tile])
-    pl.semaphore_wait(barrier, len(everyone))
-    south_copy = pltpu.make_async_remote_copy(
-        src_ref=mine, dst_ref=strip, send_sem=send.at[COPIES], recv_sem=recv.at[COPIES], device_id=south, device_id_type=MESH
-    )
+        if q == 1:
+            fold_high(mine, sums, ROWS - CUT, 2 * BAND)
+            pl.semaphore_wait(barrier, len(everyone))
+
+            @pl.when(has_south)
+            def _():
+                south_copies[0].start()
+
+    fold_high(mine, sums, 2 * BAND, CUT)
+    fold_low(mine, sums, offsets[1, own_tile])
 
     @pl.when(has_south)
     def _():
-        south_copy.start()
+        for c in south_copies[1:]:
+            c.start()
 
     @pl.when(jnp.logical_not(has_north))
     def _():
@@ -604,14 +626,16 @@
 
     @pl.when(has_north)
     def _():
-        south_copy.wait_recv()
+        for c in south_copies:
+            c.wait_recv()
 
     for c in started:
         c.wait_send()
 
     @pl.when(has_south)
     def _():
-        south_copy.wait_send()
+        for c in south_copies:
+            c.wait_send()
 
 
 COPIES = CHAINS * (2 * len(WIDTHS) + 2 + len(WIDTHS) + 1) + 1 + (2 * REACH + 2) + (2 * REACH + 1)
@@ -656,8 +680,8 @@
             pltpu.VMEM((ROWS, 2 * CUT), F32),
             pltpu.VMEM((32, 128), F32),
             pltpu.SemaphoreType.DMA((CHAINS + 1,)),
-            pltpu.SemaphoreType.DMA((COPIES + 1,)),
-            pltpu.SemaphoreType.DMA((COPIES + 1,)),
+            pltpu.SemaphoreType.DMA((COPIES + 3,)),
+            pltpu.SemaphoreType.DMA((COPIES + 3,)),
         ],
         compiler_params=pltpu.CompilerParams(collective_id=0, has_side_effects=True, vmem_limit_bytes=FIRST_LIMIT << 20),
         name="first",

time: 112 us -> 112 us (level)
  no operation moved by 1% of the time
where the time goes in v6:
time: 112 us
  Pallas kernels  109 us (97%)
  local copies, waits for them, and re-layouts  2.43 us (2%)
    pallas_call x1, Pallas kernels, body(): pl.pallas_call(first_kernel, out_shape=(shape(PLANES, ROWS, WIDTH), shape...  99.1 us
    pallas_call x1, Pallas kernels, body(): pl.pallas_call(south_kernel, out_shape=(shape(PLANES, ROWS, WIDTH), shape...  9.39 us
    unnamed x4, local copies, waits for them, and re-layouts  2.43 us

profile of v6, /device:TPU:1, one launch (start us, length us, event | category | flops | bytes accessed | tf_op | source)
XLA Modules:
  0.0 111.6 jit_solution(16166668479091991722)
XLA Ops:
  0.6 0.0 copy-start
  0.6 1.7 %copy-done = bf16[1728,768]{1,0:T(8,128)(2,1)S(1)} copy-done((bf16[1728,768]{1,0:T(8,128)(2,1)S(1)}, bf16[1728,768]{1,0:T(8,128)(2,1)}, u32[]{:S(2)}) %copy-start) | copy-done | bytes 2654232
  2.4 0.0 copy-start.1
  2.4 0.7 copy-done.1
  3.1 99.1 %first.1 = (f32[2,320,2048]{2,1,0:T(8,128)S(1)}, f32[256,2048]{1,0:T(8,128)S(1)}, f32[2304,256]{1,0:T(8,128)S(1)}, f32[320,256]{1,0:T(8,128)S(1)}, f32[256,2048]...) custom-call(s32[2,256]{1,0:T(2,128)S(1)} %bitcast.5, f32[2,320,2048]{2,1,0:T(8,128)} %bitcast.7, ...), custom_call_target="tpu_custom_call" | custom-call | tf_op jit(solution)/shard_map/first/pallas_call | solution.py:659
  102.2 9.4 %second.1 = (f32[2,320,2048]{2,1,0:T(8,128)}, f32[320,256]{1,0:T(8,128)}, f32[256,2048]{1,0:T(8,128)}) custom-call(s32[2,256]{1,0:T(2,128)S(1)} %bitcast.6, f32[2304,256]{1,0:T(8,128)S(1)} %get-tuple-element.13.own, f32[2,320,2048]{2,1,0:T(8,128)S(1)} %get-tuple-element.14.ready, f32[320,256]{1,0:T(8,128)S(1)} %get-tuple-element.15.east, ...), custom_call_target="tpu_custom_call" | custom-call | tf_op jit(solution)/shard_map/second/pallas_call | solution.py:689
Async XLA Ops:
  0.6 1.8 %copy-start = (bf16[1728,768]{1,0:T(8,128)(2,1)S(1)}, bf16[1728,768]{1,0:T(8,128)(2,1)}, u32[]{:S(2)}) copy-start(bf16[1728,768]{1,0:T(8,128)(2,1)} %constant.2.clone.bundled) | copy-start | bytes 7962628
  2.4 0.7 copy-start.1
